TPU v7x, 32 devices: a whole 2x2x4 slice. The times are simulated.
32 devices in a mesh: img: 8 (over y, x, core), tile: 4 (over z).
Axes of the slice: x: 2, y: 2, z: 4, core: 2. Of those that a mesh axis runs over, the one named last changes fastest.
Arguments:
- vit_in: bfloat16 [16, 4, 144, 768], P('img', 'tile'), may hold values from -6 to 6
- map_in: bfloat16 [16, 4, 576, 1024], P('img', 'tile'), may hold values from -6 to 6
- group_images: int32 [8], P('img'), may hold values from 1 to 2, as said below
- vit_grad_out: bfloat16 [16, 4, 144, 768], P('img', 'tile'), may hold values from -6 to 6
- map_grad_out: bfloat16 [16, 4, 576, 1024], P('img', 'tile'), may hold values from -6 to 6
- w_query: bfloat16 [768, 768], replicated, may hold values from -0.21875 to 0.21875
- w_key: bfloat16 [768, 768], replicated, may hold values from -0.21875 to 0.21875
- w_value: bfloat16 [768, 768], replicated, may hold values from -0.21875 to 0.21875
- w_out: bfloat16 [768, 768], replicated, may hold values from -2.5 to 2.5
- w_up: bfloat16 [768, 3072], replicated, may hold values from -0.21875 to 0.21875
- w_down: bfloat16 [3072, 768], replicated, may hold values from -0.109375 to 0.109375
- w_expand: bfloat16 [1024, 4096], replicated, may hold values from -0.1875 to 0.1875
- w_shrink: bfloat16 [4096, 1024], replicated, may hold values from -0.09375 to 0.09375
- w_adapt: bfloat16 [1024, 768], replicated, may hold values from -0.375 to 0.375
- gain_attn: bfloat16 [768], replicated, may hold values from 0.099609375 to 1.8984375
- gain_mlp: bfloat16 [768], replicated, may hold values from 0.099609375 to 1.8984375
- gain_conv: bfloat16 [1024], replicated, may hold values from 0.099609375 to 1.8984375
- dw_large: bfloat16 [49, 1024], replicated, may hold values from -0.875 to 0.875
- dw_small: bfloat16 [9, 768], replicated, may hold values from -2 to 2
- gate_low: bfloat16 [768], replicated, may hold values from -0.21875 to 0.21875
- gate_high: bfloat16 [768], replicated, may hold values from -0.21875 to 0.21875
Outputs:
- vit_out: bfloat16 [16, 4, 144, 768], P('img', 'tile')
- map_out: bfloat16 [16, 4, 576, 1024], P('img', 'tile')
- vit_in_grad: bfloat16 [16, 4, 144, 768], P('img', 'tile')
- map_in_grad: bfloat16 [16, 4, 576, 1024], P('img', 'tile')
- w_query_grad: float32 [768, 768], P('img', 'tile')
- w_key_grad: float32 [768, 768], P('img', 'tile')
- w_value_grad: float32 [768, 768], P('img', 'tile')
- w_out_grad: float32 [768, 768], P('img', 'tile')
- w_up_grad: float32 [768, 3072], P('img', 'tile')
- w_down_grad: float32 [3072, 768], P('img', 'tile')
- w_expand_grad: float32 [1024, 4096], P('img', 'tile')
- w_shrink_grad: float32 [4096, 1024], P('img', 'tile')
- w_adapt_grad: float32 [1024, 768], P('img', 'tile')
- gain_attn_grad: float32 [768], replicated
- gain_mlp_grad: float32 [768], replicated
- gain_conv_grad: float32 [1024], replicated
- dw_large_grad: float32 [49, 1024], replicated
- dw_small_grad: float32 [9, 768], replicated
- gate_low_grad: float32 [768], replicated
- gate_high_grad: float32 [768], replicated
Inputs may be any that keep to these rules, and one draw needn't show every extreme that they name: Group g holds its images in slots 0 to group_images[g] - 1 of its 2 slots; other slots hold no image. In every draw some group holds 2 images and some group holds 1.
All inputs are finite; a program needn't handle non-finite values.
Results may differ from a plain program's by a relative error of at most 0.018.
Values may be sent and summed in bfloat16 or wider, within the bound.
A program may use at most 320 MiB of HBM per device.

v0:
```python
from functools import partial
import math

import jax
import jax.numpy as jnp
from jax import lax
from jax.sharding import PartitionSpec as P

HEADS = 12
HDIM = 64


highest = lax.Precision.HIGHEST


def swapped(array, axis, bit):
    return lax.ppermute(array, axis, [(i, i ^ 1 << bit) for i in range(lax.axis_size(axis))])


def layer_norm(values, gain_row):
    centre = values - jnp.mean(values, axis=-1, keepdims=True)
    spread = jnp.mean(centre * centre, axis=-1, keepdims=True)
    return centre * lax.rsqrt(spread + 1e-06) * gain_row


def gelu_exact(values):
    return 0.5 * values * (1.0 + lax.erf(values * 0.7071067811865476))


def depthwise(field_map, tap_weights, radius, margin):
    kernel_side = 2 * radius + 1
    channels = tap_weights.shape[1]
    kernel = tap_weights.reshape(kernel_side, kernel_side, 1, channels)
    return lax.conv_general_dilated(
        field_map,
        kernel,
        (1, 1),
        ((margin, margin), (margin, margin)),
        dimension_numbers=("NHWC", "HWIO", "NHWC"),
        feature_group_count=channels,
        precision=highest,
    )


def pool_pairs(field_map):
    slot_count, row_count, col_count, channels = field_map.shape
    return jnp.mean(
        field_map.reshape(slot_count, row_count // 2, 2, col_count // 2, 2, channels), axis=(2, 4)
    )


def merging(residual_two, merged_tokens, gate_low, gate_high):
    gate_logit = jnp.sum(residual_two * gate_low, axis=-1, keepdims=True) + jnp.sum(
        merged_tokens * gate_high, axis=-1, keepdims=True
    )
    gate_value = 1.0 / (1.0 + jnp.exp(-gate_logit))
    return residual_two + gate_value * merged_tokens


def project(left_side, right_side):
    return jnp.einsum("...i,ij->...j", left_side, right_side, preferred_element_type=jnp.float32)


def project_back(left_side, right_side):
    return jnp.einsum("...j,ij->...i", left_side, right_side, preferred_element_type=jnp.float32)


def outer_sum(left_side, right_side):
    flat_left = left_side.reshape(-1, left_side.shape[-1])
    flat_right = right_side.reshape(-1, right_side.shape[-1])
    return lax.dot_general(
        flat_left, flat_right, (((0,), (0,)), ((), ())), preferred_element_type=jnp.float32
    )


def split_heads(rows_low):
    return rows_low.reshape(rows_low.shape[0], rows_low.shape[1], HEADS, HDIM)


def attention_scores(query_low, key_all):
    return jnp.einsum(
        "sqhd,skhd->shqk",
        split_heads(query_low),
        split_heads(key_all),
        preferred_element_type=jnp.float32,
    ) * HDIM ** (-0.5)


def add_rims(tile_field, radius):
    tile_place = lax.axis_index("tile")
    for which_bit in range(2):
        axis_dim = 2 - which_bit
        on_low = tile_place >> which_bit & 1 == 0
        side_len = tile_field.shape[axis_dim]
        upper_rim = lax.slice_in_dim(tile_field, side_len - radius, side_len, axis=axis_dim)
        lower_rim = lax.slice_in_dim(tile_field, 0, radius, axis=axis_dim)
        outgoing = jnp.where(on_low, upper_rim, lower_rim)
        incoming = swapped(outgoing, "tile", which_bit)
        blank_rim = jnp.zeros_like(incoming)
        tile_field = jnp.where(
            on_low,
            jnp.concatenate([blank_rim, tile_field, incoming], axis_dim),
            jnp.concatenate([incoming, tile_field, blank_rim], axis_dim),
        )
    return tile_field


def return_rims(grad_field, radius):
    tile_place = lax.axis_index("tile")
    for which_bit in (1, 0):
        axis_dim = 2 - which_bit
        on_low = tile_place >> which_bit & 1 == 0
        total_len = grad_field.shape[axis_dim]
        side_len = total_len - 2 * radius
        high_rim = lax.slice_in_dim(grad_field, total_len - radius, total_len, axis=axis_dim)
        low_rim = lax.slice_in_dim(grad_field, 0, radius, axis=axis_dim)
        outgoing = jnp.where(on_low, high_rim, low_rim)
        incoming = swapped(outgoing.astype(jnp.bfloat16), "tile", which_bit).astype(outgoing.dtype)
        core_part = lax.slice_in_dim(grad_field, radius, radius + side_len, axis=axis_dim)
        filler_shape = list(incoming.shape)
        filler_shape[axis_dim] = side_len - radius
        filler = jnp.zeros(filler_shape, jnp.float32)
        grad_field = core_part + jnp.where(
            on_low,
            jnp.concatenate([filler, incoming], axis_dim),
            jnp.concatenate([incoming, filler], axis_dim),
        )
    return grad_field


def gather_pair(key_low, value_low):
    return (
        lax.all_gather(key_low, "tile", axis=1, tiled=True),
        lax.all_gather(value_low, "tile", axis=1, tiled=True),
    )


def local(
    vit_in,
    map_in,
    group_images,
    vit_grad_out,
    map_grad_out,
    w_query,
    w_key,
    w_value,
    w_out,
    w_up,
    w_down,
    w_expand,
    w_shrink,
    w_adapt,
    gain_attn,
    gain_mlp,
    gain_conv,
    dw_large,
    dw_small,
    gate_low,
    gate_high,
):
    slot_count = vit_in.shape[0]
    tok_side = math.isqrt(vit_in.shape[2])
    pix_side = math.isqrt(map_in.shape[2])
    channels = map_in.shape[3]
    model_width = vit_in.shape[3]
    live_mask = (
        (jnp.arange(slot_count, dtype=jnp.int32) < group_images[0])
        .astype(jnp.float32)
        .reshape(slot_count, 1, 1)
    )
    live_cells = live_mask.reshape(slot_count, 1, 1, 1)
    tokens = vit_in[:, 0].astype(jnp.float32)
    normed_one, norm_one_pull = jax.vjp(layer_norm, tokens, gain_attn.astype(jnp.float32))
    normed_one_low = normed_one.astype(jnp.bfloat16)
    query_low = project(normed_one_low, w_query).astype(jnp.bfloat16)
    key_low = project(normed_one_low, w_key).astype(jnp.bfloat16)
    value_low = project(normed_one_low, w_value).astype(jnp.bfloat16)
    key_all, value_all = gather_pair(key_low, value_low)
    scores = attention_scores(query_low, key_all)
    row_max = jnp.max(scores, axis=-1, keepdims=True)
    shifted = jnp.exp(scores - row_max)
    row_total = jnp.sum(shifted, axis=-1, keepdims=True)
    softmax_low = (shifted / row_total).astype(jnp.bfloat16)
    log_total = row_max + jnp.log(row_total)
    mixed_low = (
        jnp.einsum(
            "shqk,skhd->sqhd",
            softmax_low,
            split_heads(value_all),
            preferred_element_type=jnp.float32,
        )
        .reshape(slot_count, -1, model_width)
        .astype(jnp.bfloat16)
    )
    residual_one = tokens + project(mixed_low, w_out)
    normed_two, norm_two_pull = jax.vjp(layer_norm, residual_one, gain_mlp.astype(jnp.float32))
    normed_two_low = normed_two.astype(jnp.bfloat16)
    acted, acted_pull = jax.vjp(gelu_exact, project(normed_two_low, w_up))
    acted_low = acted.astype(jnp.bfloat16)
    residual_two = residual_one + project(acted_low, w_down)
    map_low = map_in[:, 0].reshape(slot_count, pix_side, pix_side, channels)
    padded_map = add_rims(map_low, 3).astype(jnp.float32)
    spread_map, spread_pull = jax.vjp(
        partial(depthwise, radius=3, margin=0), padded_map, dw_large.astype(jnp.float32)
    )
    conv_norm, conv_norm_pull = jax.vjp(layer_norm, spread_map, gain_conv.astype(jnp.float32))
    conv_norm_low = conv_norm.astype(jnp.bfloat16)
    wide_act, wide_pull = jax.vjp(gelu_exact, project(conv_norm_low, w_expand))
    wide_low = wide_act.astype(jnp.bfloat16)
    map_after = map_low.astype(jnp.float32) + project(wide_low, w_shrink)
    pooled, pool_pull = jax.vjp(pool_pairs, map_after)
    pooled_low = pooled.astype(jnp.bfloat16)
    adapted_low = project(pooled_low, w_adapt).astype(jnp.bfloat16)
    padded_small = add_rims(adapted_low, 1).astype(jnp.float32)
    merged_map, merged_pull = jax.vjp(
        partial(depthwise, radius=1, margin=0), padded_small, dw_small.astype(jnp.float32)
    )
    merged_tokens = merged_map.reshape(slot_count, tok_side * tok_side, model_width)
    vit_after, merging_pull = jax.vjp(
        merging,
        residual_two,
        merged_tokens,
        gate_low.astype(jnp.float32),
        gate_high.astype(jnp.float32),
    )
    vit_cotangent = vit_grad_out[:, 0].astype(jnp.float32) * live_mask
    map_cotangent = (
        map_grad_out[:, 0].astype(jnp.float32).reshape(slot_count, pix_side, pix_side, channels)
        * live_cells
    )
    grad_residual_two, grad_merged, gate_low_grad, gate_high_grad = merging_pull(vit_cotangent)
    grad_padded_small, dw_small_grad = merged_pull(
        grad_merged.reshape(slot_count, tok_side, tok_side, model_width)
    )
    grad_adapted_low = return_rims(grad_padded_small, 1).astype(jnp.bfloat16)
    w_adapt_grad = outer_sum(pooled_low, grad_adapted_low)
    grad_map_after = map_cotangent + pool_pull(project_back(grad_adapted_low, w_adapt))[0]
    grad_conv_low = grad_map_after.astype(jnp.bfloat16)
    w_shrink_grad = outer_sum(wide_low, grad_conv_low)
    grad_wide_low = wide_pull(project_back(grad_conv_low, w_shrink))[0].astype(jnp.bfloat16)
    w_expand_grad = outer_sum(conv_norm_low, grad_wide_low)
    grad_spread, gain_conv_grad = conv_norm_pull(project_back(grad_wide_low, w_expand))
    grad_padded_map, dw_large_grad = spread_pull(grad_spread)
    map_in_grad = (grad_map_after + return_rims(grad_padded_map, 3)).astype(jnp.bfloat16)
    grad_mlp_low = grad_residual_two.astype(jnp.bfloat16)
    w_down_grad = outer_sum(acted_low, grad_mlp_low)
    grad_up_low = acted_pull(project_back(grad_mlp_low, w_down))[0].astype(jnp.bfloat16)
    w_up_grad = outer_sum(normed_two_low, grad_up_low)
    grad_norm_part, gain_mlp_grad = norm_two_pull(project_back(grad_up_low, w_up))
    grad_residual_one = grad_residual_two + grad_norm_part
    grad_attn_low = grad_residual_one.astype(jnp.bfloat16)
    w_out_grad = outer_sum(mixed_low, grad_attn_low)
    grad_mixed_low = project_back(grad_attn_low, w_out).astype(jnp.bfloat16)
    key_back, value_back = (key_all, value_all)
    softmax_again = jnp.exp(attention_scores(query_low, key_back) - log_total)
    softmax_again_low = softmax_again.astype(jnp.bfloat16)
    grad_mixed_heads = split_heads(grad_mixed_low)
    grad_softmax = jnp.einsum(
        "sqhd,skhd->shqk",
        grad_mixed_heads,
        split_heads(value_back),
        preferred_element_type=jnp.float32,
    )
    row_dot = jnp.sum(softmax_again * grad_softmax, axis=-1, keepdims=True)
    grad_scores_low = (softmax_again * (grad_softmax - row_dot)).astype(jnp.bfloat16)
    scale = HDIM ** (-0.5)
    grad_query_low = (
        (
            jnp.einsum(
                "shqk,skhd->sqhd",
                grad_scores_low,
                split_heads(key_back),
                preferred_element_type=jnp.float32,
            )
            * scale
        )
        .reshape(slot_count, -1, model_width)
        .astype(jnp.bfloat16)
    )
    grad_key_term = (
        jnp.einsum(
            "shqk,sqhd->skhd",
            grad_scores_low,
            split_heads(query_low),
            preferred_element_type=jnp.float32,
        )
        * scale
    ).reshape(slot_count, -1, model_width)
    grad_value_term = jnp.einsum(
        "shqk,sqhd->skhd", softmax_again_low, grad_mixed_heads, preferred_element_type=jnp.float32
    ).reshape(slot_count, -1, model_width)
    grad_key_sum, grad_value_sum = (
        lax.psum_scatter(
            grad_key_term.astype(jnp.bfloat16), "tile", scatter_dimension=1, tiled=True
        ).astype(jnp.float32),
        lax.psum_scatter(
            grad_value_term.astype(jnp.bfloat16), "tile", scatter_dimension=1, tiled=True
        ).astype(jnp.float32),
    )
    grad_key_low = grad_key_sum.astype(jnp.bfloat16)
    grad_value_low = grad_value_sum.astype(jnp.bfloat16)
    w_query_grad = outer_sum(normed_one_low, grad_query_low)
    w_key_grad = outer_sum(normed_one_low, grad_key_low)
    w_value_grad = outer_sum(normed_one_low, grad_value_low)
    grad_normed_one = (
        project_back(grad_query_low, w_query)
        + project_back(grad_key_low, w_key)
        + project_back(grad_value_low, w_value)
    )
    grad_token_part, gain_attn_grad = norm_one_pull(grad_normed_one)
    vit_in_grad = (grad_residual_one + grad_token_part).astype(jnp.bfloat16)
    by_group = (
        lax.psum_scatter(w_query_grad, "img", scatter_dimension=0, tiled=True),
        lax.psum_scatter(w_key_grad, "img", scatter_dimension=0, tiled=True),
        lax.psum_scatter(w_value_grad, "img", scatter_dimension=0, tiled=True),
        lax.psum_scatter(w_out_grad, "img", scatter_dimension=0, tiled=True),
        lax.psum_scatter(w_up_grad, "img", scatter_dimension=0, tiled=True),
        lax.psum_scatter(w_down_grad, "img", scatter_dimension=0, tiled=True),
        lax.psum_scatter(w_expand_grad, "img", scatter_dimension=0, tiled=True),
        lax.psum_scatter(w_shrink_grad, "img", scatter_dimension=0, tiled=True),
        lax.psum_scatter(w_adapt_grad, "img", scatter_dimension=0, tiled=True),
    )
    matrix_sums = (
        lax.psum_scatter(
            by_group[0].astype(jnp.bfloat16), "tile", scatter_dimension=1, tiled=True
        ).astype(jnp.float32),
        lax.psum_scatter(
            by_group[1].astype(jnp.bfloat16), "tile", scatter_dimension=1, tiled=True
        ).astype(jnp.float32),
        lax.psum_scatter(
            by_group[2].astype(jnp.bfloat16), "tile", scatter_dimension=1, tiled=True
        ).astype(jnp.float32),
        lax.psum_scatter(
            by_group[3].astype(jnp.bfloat16), "tile", scatter_dimension=1, tiled=True
        ).astype(jnp.float32),
        lax.psum_scatter(
            by_group[4].astype(jnp.bfloat16), "tile", scatter_dimension=1, tiled=True
        ).astype(jnp.float32),
        lax.psum_scatter(
            by_group[5].astype(jnp.bfloat16), "tile", scatter_dimension=1, tiled=True
        ).astype(jnp.float32),
        lax.psum_scatter(
            by_group[6].astype(jnp.bfloat16), "tile", scatter_dimension=1, tiled=True
        ).astype(jnp.float32),
        lax.psum_scatter(
            by_group[7].astype(jnp.bfloat16), "tile", scatter_dimension=1, tiled=True
        ).astype(jnp.float32),
        lax.psum_scatter(
            by_group[8].astype(jnp.bfloat16), "tile", scatter_dimension=1, tiled=True
        ).astype(jnp.float32),
    )
    small_sums = lax.psum(
        (
            gain_attn_grad,
            gain_mlp_grad,
            gain_conv_grad,
            dw_large_grad,
            dw_small_grad,
            gate_low_grad,
            gate_high_grad,
        ),
        ("img", "tile"),
    )
    vit_result = (vit_after * live_mask).astype(jnp.bfloat16)[:, None]
    map_result = (
        (map_after * live_cells)
        .reshape(slot_count, pix_side * pix_side, channels)
        .astype(jnp.bfloat16)[:, None]
    )
    return (
        vit_result,
        map_result,
        vit_in_grad[:, None],
        map_in_grad.reshape(slot_count, pix_side * pix_side, channels)[:, None],
        matrix_sums[0],
        matrix_sums[1],
        matrix_sums[2],
        matrix_sums[3],
        matrix_sums[4],
        matrix_sums[5],
        matrix_sums[6],
        matrix_sums[7],
        matrix_sums[8],
        small_sums[0],
        small_sums[1],
        small_sums[2],
        small_sums[3],
        small_sums[4],
        small_sums[5],
        small_sums[6],
    )


def solution(mesh):
    in_specs = (
        P("img", "tile", None, None),
        P("img", "tile", None, None),
        P("img"),
        P("img", "tile", None, None),
        P("img", "tile", None, None),
        P(),
        P(),
        P(),
        P(),
        P(),
        P(),
        P(),
        P(),
        P(),
        P(),
        P(),
        P(),
        P(),
        P(),
        P(),
        P(),
    )
    out_specs = (
        P("img", "tile", None, None),
        P("img", "tile", None, None),
        P("img", "tile", None, None),
        P("img", "tile", None, None),
        P("img", "tile"),
        P("img", "tile"),
        P("img", "tile"),
        P("img", "tile"),
        P("img", "tile"),
        P("img", "tile"),
        P("img", "tile"),
        P("img", "tile"),
        P("img", "tile"),
        P(),
        P(),
        P(),
        P(),
        P(),
        P(),
        P(),
    )
    return jax.shard_map(local, mesh=mesh, in_specs=in_specs, out_specs=out_specs, check_vma=False)
```

profile of v0, /device:TPU:0, one launch (start us, length us, event | category | flops | bytes accessed | tf_op | source)
XLA Modules:
  0.0 1296.1 jit_solution(6205249807614755326)
XLA Ops:
  18.7 11.7 collective-permute-done
  37.6 7.7 collective-permute-start.1
  48.5 25.3 %collective-permute-done.1 = bf16[2,3,30,1024]{3,2,1,0:T(8,128)(2,1)} collective-permute-done((bf16[2,3,30,1024]{3,2,1,0:T(8,128)(2,1)}, bf16[2,3,30,1024]{3,2,1,0:T(8,128)(2,1)}, u32[]{:S(2)}, u32[]{:S(2)}) %collective-permute-start.1) | collective-permute-done | bytes 368672 | tf_op jit(solution)/shard_map/ppermute | solution.py:17
  76.4 31.0 %fusion.143 = (f32[2,24,24]{0,2,1:T(8,128)S(1)}, f32[2,24,24,1024]{3,0,2,1:T(2,128)}) fusion(bf16[7,7,1,1024]{3,2,1,0:T(2,128)(2,1)S(1)} %reshape.334, bf16[2,30,30,1024]{3,2,1,0:T(8,128)(2,1)S(1)} %maximum_select_fusion), kind=kOutput, calls=%fused_computation.217 | convolution fusion | flops 116784000 | bytes 8509952 | tf_op jit(solution)/shard_map/jvp()/conv_general_dilated | solution.py:34
  107.9 5.1 multiply_reduce_fusion.4
  113.4 5.1 multiply_convert_fusion.3
  118.6 17.1 %multiply_convert_fusion = (bf16[2,24,24,4096]{3,2,1,0:T(8,128)(2,1)S(1)}, f32[2,24,24,4096]{3,2,1,0:T(8,128)}) fusion(bf16[1024,4096]{1,0:T(8,128)(2,1)} %param.32, bf16[2,24,24,1024]{3,0,2,1:T(2,128)(2,1)S(1)} %multiply_convert_fusion.3), kind=kOutput, calls=%fused_computation.1 | convolution fusion | flops 9687269376 | bytes 39059456 | tf_op jit(solution)/shard_map/...i,ij->...j/dot_general | solution.py:61
  139.3 12.1 convert_add_fusion
  151.4 6.7 reshape.290
  158.2 7.3 reduce_sum.225
  199.0 6.4 fusion.58
  210.2 4.7 multiply_reduce_fusion.11
  215.0 6.6 add_convert_fusion.1
  230.8 7.1 fusion.45
  237.9 4.0 copy.240
  241.9 7.3 multiply_reduce_fusion
  249.2 5.4 multiply_convert_fusion.1
  258.8 3.9 copy.239
  266.7 4.2 multiply_convert_fusion.6
  292.9 7.1 collective-permute-done.5
  300.1 4.3 convolution_bitcast_fusion.4
  308.0 13.5 %reduce-scatter.33.cloned.1.call-done = bf16[2,144,768]{2,1,0:T(8,128)(2,1)} async-done(((bf16[2,576,768]{2,1,0:T(8,128)(2,1)}), bf16[2,144,768]{2,1,0:T(8,128)(2,1)}) %reduce-scatter.33.cloned.1.call-update) | async-done | bytes 442384 | tf_op jit(solution)/shard_map/reduce_scatter | solution.py:293
  325.0 7.8 convolution_bitcast_fusion.2
  334.1 6.8 convolution_bitcast_fusion.3
  343.0 4.4 broadcast_in_dim.78
  347.4 7.0 reshape.295
  354.3 4.0 fusion.34
  358.4 21.1 %add_convert_fusion = bf16[2,24,24,4096]{3,2,1,0:T(8,128)(2,1)S(1)} fusion(f32[2,24,24,4096]{3,2,1,0:T(8,128)} %get-tuple-element.158, bf16[2,24,24,1024]{3,2,1,0:T(8,128)(2,1)S(1)} %fusion.34, bf16[4096,1024]{1,0:T(8,128)(2,1)} %param.33), kind=kOutput, calls=%fused_computation | convolution fusion | flops 9725018112 | bytes 39059456 | tf_op jit(solution)/shard_map/...j,ij->...i/dot_general | solution.py:65
  383.2 15.1 %convolution_bitcast_fusion.1 = f32[1024,4096]{1,0:T(8,128)} fusion(bf16[2,24,24,4096]{3,2,1,0:T(8,128)(2,1)S(1)} %add_convert_fusion, bf16[2,24,24,1024]{3,0,2,1:T(2,128)(2,1)S(1)} %copy-done.34), kind=kOutput, calls=%fused_computation.9 | convolution fusion | flops 9663676416 | bytes 28573696 | tf_op jit(solution)/shard_map/dot_general | solution.py:71
  398.7 17.8 %convolution_bitcast_fusion = f32[4096,1024]{1,0:T(8,128)} fusion(bf16[2,24,24,4096]{3,2,1,0:T(8,128)(2,1)} %copy-done.105, bf16[2,24,24,1024]{3,2,1,0:T(8,128)(2,1)} %copy-done.35), kind=kOutput, calls=%fused_computation.8 | convolution fusion | flops 9663676416 | bytes 28573696 | tf_op jit(solution)/shard_map/dot_general | solution.py:71
  420.4 42.5 %reduce-scatter.59.cloned.1.call-done = f32[128,768]{1,0:T(8,128)} async-done(((f32[1024,768]{1,0:T(8,128)}), f32[128,768]{1,0:T(8,128)}) %reduce-scatter.59.cloned.1.call-update) | async-done | bytes 393232 | tf_op jit(solution)/shard_map/reduce_scatter | solution.py:321
  464.9 44.2 %reduce-scatter.41.cloned.1.call-done = f32[96,768]{1,0:T(8,128)} async-done(((f32[768,768]{1,0:T(8,128)}), f32[96,768]{1,0:T(8,128)}) %reduce-scatter.41.cloned.1.call-update) | async-done | bytes 294928 | tf_op jit(solution)/shard_map/reduce_scatter | solution.py:315
  511.1 15.9 %fusion = f32[2,24,24,1024]{3,2,1,0:T(8,128)} fusion(bf16[2,24,24,4096]{3,2,1,0:T(8,128)(2,1)} %copy-done.104, bf16[1024,4096]{1,0:T(8,128)(2,1)} %param.32), kind=kOutput, calls=%fused_computation.10 | convolution fusion | flops 9663676416 | bytes 22544384 | tf_op jit(solution)/shard_map/...j,ij->...i/dot_general | solution.py:65
  527.0 28.6 %reduce-scatter.39.cloned.1.call-done = f32[96,768]{1,0:T(8,128)} async-done(((f32[768,768]{1,0:T(8,128)}), f32[96,768]{1,0:T(8,128)}) %reduce-scatter.39.cloned.1.call-update) | async-done | bytes 294928 | tf_op jit(solution)/shard_map/reduce_scatter | solution.py:314
  557.7 12.6 multiply_reduce_fusion.2
  570.7 65.2 %reduce-scatter.49.cloned.1.call-done = f32[384,768]{1,0:T(8,128)} async-done(((f32[3072,768]{1,0:T(8,128)}), f32[384,768]{1,0:T(8,128)}) %reduce-scatter.49.cloned.1.call-update) | async-done | bytes 1179664 | tf_op jit(solution)/shard_map/reduce_scatter | solution.py:318
  638.3 11.6 fusion.140
  650.4 7.5 fusion.181
  657.9 58.4 %reduce-scatter.45.cloned.1.call-done = f32[96,3072]{1,0:T(8,128)} async-done(((f32[768,3072]{1,0:T(8,128)}), f32[96,3072]{1,0:T(8,128)}) %reduce-scatter.45.cloned.1.call-update) | async-done | bytes 1179664 | tf_op jit(solution)/shard_map/reduce_scatter | solution.py:317
  718.5 45.0 %fusion.27 = f32[2,30,30,1024]{3,0,2,1:T(2,128)} fusion(bf16[7,7,1024,1]{2,3,1,0:T(2,128)(2,1)S(1)} %reshape.337, f32[2,24,24,1024]{3,0,2,1:T(2,128)} %fusion.181), kind=kOutput, calls=%fused_computation.53 | convolution fusion | flops 693633024 | bytes 12191744 | tf_op jit(solution)/shard_map/transpose(jvp())/conv_general_dilated | solution.py:34
  763.5 72.6 %reduce-scatter.51.cloned.1.call-done = f32[128,4096]{1,0:T(8,128)} async-done(((f32[1024,4096]{1,0:T(8,128)}), f32[128,4096]{1,0:T(8,128)}) %reduce-scatter.51.cloned.1.call-update) | async-done | bytes 2097168 | tf_op jit(solution)/shard_map/reduce_scatter | solution.py:319
  844.5 4.7 convolution_reduce_fusion
  851.6 10.9 collective-permute-done.6
  869.3 86.8 %reduce-scatter.55.cloned.1.call-done = f32[512,1024]{1,0:T(8,128)} async-done(((f32[4096,1024]{1,0:T(8,128)}), f32[512,1024]{1,0:T(8,128)}) %reduce-scatter.55.cloned.1.call-update) | async-done | bytes 2097168 | tf_op jit(solution)/shard_map/reduce_scatter | solution.py:320
  958.9 127.6 %fusion.79 = f32[7,7,1024]{2,1,0:T(8,128)S(1)} fusion(f32[2,24,24,1024]{3,0,2,1:T(2,128)} %get-tuple-element.135, f32[2,24,24]{0,2,1:T(8,128)S(1)} %copy.255, bf16[2,30,30,1024]{3,2,1,0:T(8,128)(2,1)} %copy-done.22), kind=kOutput, calls=%fused_computation.118 | convolution fusion | flops 694812672 | bytes 8610304 | tf_op jit(solution)/shard_map/transpose(jvp())/conv_general_dilated | solution.py:34
  1087.4 9.8 fusion.10
  1101.0 42.7 %all-reduce.8 = (f32[768]{0:T(1024)}, f32[768]{0:T(1024)}, f32[1024]{0:T(1024)}, f32[9,768]{1,0:T(8,128)}, f32[768]{0:T(1024)}, /*index=5*/f32[768]{0:T(1024)}) all-reduce(f32[768]{0:T(1024)S(1)} %get-tuple-element.124, f32[768]{0:T(1024)S(1)} %copy-done.81, ...), channel_id=1, replica_groups=mesh['img'=8,'tile'=4] {'img','tile'}, use_global_device_ids=true, to_apply=%region_40.41 | all-reduce | flops 11008 | bytes 88064 | tf_op jit(solution)/shard_map/psum | solution.py:352
  1161.6 126.2 %all-reduce.11.cloned.1.call-done = f32[49,1024]{1,0:T(8,128)} async-done(((f32[49,1024]{1,0:T(8,128)}), f32[49,1024]{1,0:T(8,128)}) %all-reduce.11.cloned.1.call-update) | async-done | bytes 200720 | tf_op jit(solution)/shard_map/psum | solution.py:352
  (437 shorter events, 179.2 us)
Async XLA Ops:
  7.2 158.3 %copy-start = (bf16[1024,768]{1,0:T(8,128)(2,1)S(1)}, bf16[1024,768]{1,0:T(8,128)(2,1)}, u32[]{:S(2)}) copy-start(bf16[1024,768]{1,0:T(8,128)(2,1)} %param.34) | copy-start | bytes 4718596
  7.2 177.7 %all-gather.5.cloned.1.call-start = ((), (), s32[]{:S(2)}) async-start(), calls=%async_computation.21 | async-start | bytes 2211840 | tf_op jit(solution)/shard_map/all_gather | solution.py:133
  8.5 38.6 %copy-start.69 = (f32[2,144]{1,0:T(2,128)}, f32[2,144]{1,0:T(2,128)S(1)}, u32[]{:S(2)}) copy-start(f32[2,144]{1,0:T(2,128)S(1)} %broadcast_multiply_fusion.2) | copy-start | bytes 3460
  10.4 36.7 %copy-start.77 = (f32[2,144]{1,0:T(2,128)}, f32[2,144]{1,0:T(2,128)S(1)}, u32[]{:S(2)}) copy-start(f32[2,144]{1,0:T(2,128)S(1)} %fusion.127) | copy-start | bytes 3460
  11.1 36.0 %copy-start.66 = (f32[768]{0:T(1024)}, f32[768]{0:T(1024)S(1)}, u32[]{:S(2)}) copy-start(f32[768]{0:T(1024)S(1)} %convert_element_type.269) | copy-start | bytes 9220
  13.9 181.2 %all-gather.3.cloned.1.call-start = ((), (), s32[]{:S(2)}) async-start(), calls=%async_computation.20 | async-start | bytes 2211840 | tf_op jit(solution)/shard_map/all_gather | solution.py:134
  15.6 14.8 %collective-permute-start = (bf16[2,24,3,1024]{3,2,1,0:T(4,128)(2,1)S(1)}, bf16[2,24,3,1024]{3,2,1,0:T(4,128)(2,1)S(1)}, u32[]{:S(2)}, u32[]{:S(2)}) collective-permute-start(bf16[2,24,3,1024]{3,2,1,0:T(4,128)(2,1)S(1)} %slice_select_fusion.2), channel_id=1, source_target_pairs={{0,1},{1,0},{2,3},{3,2},{4,5},{5,4},{6,7},{7,6},{8,9},{9,8},{10,11... | collective-permute-start | bytes 884744 | tf_op jit(solution)/shard_map/ppermute | solution.py:17
  18.7 26.6 %copy-start.6 = (bf16[2,1,144,768]{3,2,1,0:T(8,128)(2,1)S(1)}, bf16[2,1,144,768]{3,2,1,0:T(8,128)(2,1)}, u32[]{:S(2)}) copy-start(bf16[2,1,144,768]{3,2,1,0:T(8,128)(2,1)} %param.21) | copy-start | bytes 1327108
  18.7 26.6 %copy-start.44 = (bf16[768,768]{1,0:T(8,128)(2,1)S(1)}, bf16[768,768]{1,0:T(8,128)(2,1)}, u32[]{:S(2)}) copy-start(bf16[768,768]{1,0:T(8,128)(2,1)} %param.28) | copy-start | bytes 3538948
  37.6 36.2 %collective-permute-start.1 = (bf16[2,3,30,1024]{3,2,1,0:T(8,128)(2,1)}, bf16[2,3,30,1024]{3,2,1,0:T(8,128)(2,1)}, u32[]{:S(2)}, u32[]{:S(2)}) collective-permute-start(bf16[2,3,30,1024]{3,2,1,0:T(8,128)(2,1)} %slice_select_fusion.1), channel_id=1, source_target_pairs={{0,2},{1,3},{2,0},{3,1},{4,6},{5,7},{6,4},{7,5},{8,10},{9,11},{10,... | collective-permute-start | bytes 1105928 | tf_op jit(solution)/shard_map/ppermute | solution.py:17
  46.6 257.8 %reduce-scatter.35.cloned.1.call-start = ((), (), s32[]{:S(2)}) async-start(), calls=%async_computation.23 | async-start | bytes 2211840 | tf_op jit(solution)/shard_map/reduce_scatter | solution.py:296
  47.0 66.4 %copy-start.64 = (f32[1024]{0:T(1024)}, f32[1024]{0:T(1024)S(1)}, u32[]{:S(2)}) copy-start(f32[1024]{0:T(1024)S(1)} %convert_element_type.283) | copy-start | bytes 12292
  76.4 31.0 %copy-start.22 = (bf16[2,30,30,1024]{3,2,1,0:T(8,128)(2,1)}, bf16[2,30,30,1024]{3,2,1,0:T(8,128)(2,1)S(1)}, u32[]{:S(2)}) copy-start(bf16[2,30,30,1024]{3,2,1,0:T(8,128)(2,1)S(1)} %maximum_select_fusion) | copy-start | bytes 11059204
  113.4 25.9 %slice-start.1 = ((s8[8388608]{0:T(1024)(128)(4,1)}), s8[4194304]{0:T(1024)(128)(4,1)S(1)}, s32[]{:S(2)}) async-start(s8[8388608]{0:T(1024)(128)(4,1)} %bitcast.314), calls=%async_computation.44 | async-start | bytes 8388608
  167.9 4.4 collective-permute-start.2
  173.6 5.3 collective-permute-start.3
  241.9 79.7 %reduce-scatter.33.cloned.1.call-start = ((), (), s32[]{:S(2)}) async-start(), calls=%async_computation.22 | async-start | bytes 2211840 | tf_op jit(solution)/shard_map/reduce_scatter | solution.py:293
  262.7 153.9 %reduce-scatter.43.cloned.1.call-start = ((), (), s32[]{:S(2)}) async-start(), calls=%async_computation.27 | async-start | bytes 2654208 | tf_op jit(solution)/shard_map/reduce_scatter | solution.py:316
  266.4 152.1 %reduce-scatter.37.cloned.1.call-start = ((), (), s32[]{:S(2)}) async-start(), calls=%async_computation.24 | async-start | bytes 2654208 | tf_op jit(solution)/shard_map/reduce_scatter | solution.py:313
  274.2 188.7 %reduce-scatter.59.cloned.1.call-start = ((), (), s32[]{:S(2)}) async-start(), calls=%async_computation.35 | async-start | bytes 3538944 | tf_op jit(solution)/shard_map/reduce_scatter | solution.py:321
  285.6 5.7 collective-permute-start.4
  292.8 7.2 collective-permute-start.5
  304.4 204.8 %reduce-scatter.41.cloned.1.call-start = ((), (), s32[]{:S(2)}) async-start(), calls=%async_computation.26 | async-start | bytes 2654208 | tf_op jit(solution)/shard_map/reduce_scatter | solution.py:315
  308.0 247.6 %reduce-scatter.39.cloned.1.call-start = ((), (), s32[]{:S(2)}) async-start(), calls=%async_computation.25 | async-start | bytes 2654208 | tf_op jit(solution)/shard_map/reduce_scatter | solution.py:314
  324.9 310.9 %reduce-scatter.49.cloned.1.call-start = ((), (), s32[]{:S(2)}) async-start(), calls=%async_computation.30 | async-start | bytes 10616832 | tf_op jit(solution)/shard_map/reduce_scatter | solution.py:318
  332.9 383.4 %reduce-scatter.45.cloned.1.call-start = ((), (), s32[]{:S(2)}) async-start(), calls=%async_computation.28 | async-start | bytes 10616832 | tf_op jit(solution)/shard_map/reduce_scatter | solution.py:317
  340.9 495.2 %reduce-scatter.51.cloned.1.call-start = ((), (), s32[]{:S(2)}) async-start(), calls=%async_computation.31 | async-start | bytes 18874368 | tf_op jit(solution)/shard_map/reduce_scatter | solution.py:319
  358.4 24.8 %copy-start.34 = (bf16[2,24,24,1024]{3,0,2,1:T(2,128)(2,1)S(1)}, bf16[2,24,24,1024]{3,0,2,1:T(2,128)(2,1)}, u32[]{:S(2)}) copy-start(bf16[2,24,24,1024]{3,0,2,1:T(2,128)(2,1)} %copy-done.33) | copy-start | bytes 7077892
  398.2 557.8 %reduce-scatter.55.cloned.1.call-start = ((), (), s32[]{:S(2)}) async-start(), calls=%async_computation.33 | async-start | bytes 18874368 | tf_op jit(solution)/shard_map/reduce_scatter | solution.py:320
  416.5 48.3 %copy-start.49 = (bf16[49,1024]{1,0:T(8,128)(2,1)S(1)}, bf16[49,1024]{1,0:T(8,128)(2,1)}, u32[]{:S(2)}) copy-start(bf16[49,1024]{1,0:T(8,128)(2,1)} %param.38) | copy-start | bytes 301060
  416.5 727.2 %reduce-scatter.67.cloned.1.call-start = ((), (), s32[]{:S(2)}) async-start(), calls=%async_computation.40 | async-start | bytes 245760
  418.4 726.9 %reduce-scatter.61.cloned.1.call-start = ((), (), s32[]{:S(2)}) async-start(), calls=%async_computation.37 | async-start | bytes 245760
  420.3 726.5 %reduce-scatter.71.cloned.1.call-start = ((), (), s32[]{:S(2)}) async-start(), calls=%async_computation.42 | async-start | bytes 245760
  464.8 683.7 %reduce-scatter.65.cloned.1.call-start = ((), (), s32[]{:S(2)}) async-start(), calls=%async_computation.39 | async-start | bytes 245760
  511.0 46.7 %copy-start.16 = (f32[2,24,24]{0,2,1:T(8,128)S(1)}, f32[2,24,24]{0,2,1:T(8,128)}, u32[]{:S(2)}) copy-start(f32[2,24,24]{0,2,1:T(8,128)} %copy-done.15) | copy-start | bytes 13828
  511.0 46.7 %copy-start.20 = (f32[2,24,24]{0,2,1:T(8,128)S(1)}, f32[2,24,24]{0,2,1:T(8,128)}, u32[]{:S(2)}) copy-start(f32[2,24,24]{0,2,1:T(8,128)} %copy-done.19) | copy-start | bytes 13828
  511.0 46.7 %copy-start.65 = (f32[1024]{0:T(1024)S(1)}, f32[1024]{0:T(1024)}, u32[]{:S(2)}) copy-start(f32[1024]{0:T(1024)} %copy-done.64) | copy-start | bytes 12292
  511.0 639.0 %reduce-scatter.63.cloned.1.call-start = ((), (), s32[]{:S(2)}) async-start(), calls=%async_computation.38 | async-start | bytes 245760
  557.4 594.2 %reduce-scatter.69.cloned.1.call-start = ((), (), s32[]{:S(2)}) async-start(), calls=%async_computation.41 | async-start | bytes 737280
  638.3 515.2 %reduce-scatter.47.cloned.1.call-start = ((), (), s32[]{:S(2)}) async-start(), calls=%async_computation.29 | async-start | bytes 737280 | tf_op jit(solution)/shard_map/reduce_scatter | solution.py:336
  718.5 436.7 %reduce-scatter.53.cloned.1.call-start = ((), (), s32[]{:S(2)}) async-start(), calls=%async_computation.32 | async-start | bytes 1310720 | tf_op jit(solution)/shard_map/reduce_scatter | solution.py:342
  763.5 80.9 %copy-start.24 = (f32[2,12,12,768]{3,0,2,1:T(2,128)S(1)}, f32[2,12,12,768]{3,0,2,1:T(2,128)}, u32[]{:S(2)}) copy-start(f32[2,12,12,768]{3,0,2,1:T(2,128)} %copy-done.23) | copy-start | bytes 2654212
  838.9 321.0 %reduce-scatter.57.cloned.1.call-start = ((), (), s32[]{:S(2)}) async-start(), calls=%async_computation.34 | async-start | bytes 1310720 | tf_op jit(solution)/shard_map/reduce_scatter | solution.py:345
  842.1 20.5 %collective-permute-start.6 = (bf16[2,3,30,1024]{3,2,1,0:T(8,128)(2,1)}, bf16[2,3,30,1024]{3,2,1,0:T(8,128)(2,1)}, u32[]{:S(2)}, u32[]{:S(2)}) collective-permute-start(bf16[2,3,30,1024]{3,2,1,0:T(8,128)(2,1)} %fusion.103), channel_id=1, source_target_pairs={{0,2},{1,3},{2,0},{3,1},{4,6},{5,7},{6,4},{7,5},{8,10},{9,11},{10,... | collective-permute-start | bytes 1105928 | tf_op jit(solution)/shard_map/ppermute | solution.py:17
  868.6 218.7 %collective-permute-start.7 = (bf16[2,24,3,1024]{3,2,1,0:T(4,128)(2,1)S(1)}, bf16[2,24,3,1024]{3,2,1,0:T(4,128)(2,1)S(1)}, u32[]{:S(2)}, u32[]{:S(2)}) collective-permute-start(bf16[2,24,3,1024]{3,2,1,0:T(4,128)(2,1)S(1)} %fusion.102), channel_id=1, source_target_pairs={{0,1},{1,0},{2,3},{3,2},{4,5},{5,4},{6,7},{7,6},{8,9},{9,8},{10,11... | collective-permute-start | bytes 884744 | tf_op jit(solution)/shard_map/ppermute | solution.py:17
  958.9 128.5 %copy-start.91 = (f32[2]{0:T(128)S(1)}, f32[2]{0:T(128)}, u32[]{:S(2)}) copy-start(f32[2]{0:T(128)} %copy-done.88) | copy-start | bytes 28
  958.9 328.9 %all-reduce.11.cloned.1.call-start = ((), (), s32[]{:S(2)}) async-start(), calls=%async_computation.36 | async-start | bytes 458752 | tf_op jit(solution)/shard_map/psum | solution.py:352
  1099.3 190.1 %copy-start.1 = (bf16[1024,768]{1,0:T(8,128)(2,1)S(1)}, bf16[1024,768]{1,0:T(8,128)(2,1)}, u32[]{:S(2)}) copy-start(bf16[1024,768]{1,0:T(8,128)(2,1)} %param.34) | copy-start | bytes 4718596
  (94 other events, 684.3 us)
Sparse Core Ops, SparseCore 0:
  14.0 59.1 all-gather.4
  75.3 38.4 all-gather.2
  242.0 37.3 reduce-scatter.34
  282.3 39.2 reduce-scatter.32
  324.8 41.8 reduce-scatter.42
  370.8 42.4 reduce-scatter.36
  416.7 46.2 reduce-scatter.58
  466.6 42.4 reduce-scatter.40
  513.1 42.4 reduce-scatter.38
  559.3 76.4 reduce-scatter.48
  639.8 76.4 reduce-scatter.44
  720.1 115.9 reduce-scatter.50
  840.1 115.9 reduce-scatter.54
  958.3 19.3 reduce-scatter.66
  980.4 17.5 reduce-scatter.60
  1000.1 17.5 reduce-scatter.70
  1019.8 17.5 reduce-scatter.64
  1040.2 17.5 reduce-scatter.62
  1060.1 20.1 reduce-scatter.68
  1082.5 20.3 reduce-scatter.46
  1105.2 26.1 reduce-scatter.52
  1133.8 26.0 reduce-scatter.56
  1166.0 121.7 all-reduce.10
where the time goes:
time: 1300 us
  waiting for transfers between devices  605 us (47%)
  matrix products  403 us (31%)
  other arithmetic  124 us (10%)
  local copies, waits for them, and re-layouts  87.6 us (7%)
  blocking collectives  42.7 us (3%)
  starting transfers between devices  17 us (1%)
  between operations  16.6 us (1%)
    conv_general_dilated x6, matrix products, depthwise(): lax.conv_general_dilated(field_map, kernel, (1, 1), ((margin, margin), (m...  213 us
    psum x1, waiting for transfers between devices, local(): lax.psum((gain_attn_grad, gain_mlp_grad, gain_conv_grad, dw_large_grad, d...  126 us
    reduce_scatter x1, waiting for transfers between devices, local(): lax.psum_scatter(w_shrink_grad, 'img', scatter_dimension=0, tiled=True)  86.8 us
    reduce_scatter x1, waiting for transfers between devices, local(): lax.psum_scatter(w_expand_grad, 'img', scatter_dimension=0, tiled=True)  72.6 us
    reduce_scatter x1, waiting for transfers between devices, local(): lax.psum_scatter(w_down_grad, 'img', scatter_dimension=0, tiled=True)  65.2 us
    dot_general x9, matrix products, outer_sum(): lax.dot_general(flat_left, flat_right, (((0,), (0,)), ((), ())), preferre...  64.6 us
    ppermute x8, waiting for transfers between devices, swapped(): lax.ppermute(array, axis, [(i, i ^ 1 << bit) for i in range(lax.axis_size...  63.8 us
    reduce_scatter x1, waiting for transfers between devices, local(): lax.psum_scatter(w_up_grad, 'img', scatter_dimension=0, tiled=True)  58.4 us
  transfers between devices with their start and end apart: 31, of which 17 were waited for; matrix products, arithmetic and copies ran while one was open for 42% of the time, Pallas kernels for 0%

commit v1 on v0

--- a/solution.py
+++ b/solution.py
@@ -4,6 +4,8 @@
 import jax
 import jax.numpy as jnp
 from jax import lax
+from jax.experimental import pallas as pl
+from jax.experimental.pallas import tpu as pltpu
 from jax.sharding import PartitionSpec as P
 
 HEADS = 12
@@ -25,6 +27,12 @@
 
 def gelu_exact(values):
     return 0.5 * values * (1.0 + lax.erf(values * 0.7071067811865476))
+
+
+def gelu_pair(values):
+    spread = 0.5 * (1.0 + lax.erf(values * 0.7071067811865476))
+    bell = jnp.exp(-0.5 * values * values) * 0.3989422804014327
+    return (values * spread).astype(jnp.bfloat16), (spread + values * bell).astype(jnp.bfloat16)
 
 
 def depthwise(field_map, tap_weights, radius, margin):
@@ -70,7 +78,7 @@
     flat_right = right_side.reshape(-1, right_side.shape[-1])
     return lax.dot_general(
         flat_left, flat_right, (((0,), (0,)), ((), ())), preferred_element_type=jnp.float32
-    )
+    ).astype(jnp.bfloat16)
 
 
 def split_heads(rows_low):
@@ -133,6 +141,452 @@
         lax.all_gather(key_low, "tile", axis=1, tiled=True),
         lax.all_gather(value_low, "tile", axis=1, tiled=True),
     )
+
+
+MESH = pl.DeviceIdType.MESH
+VMEM_LIMIT = 60 << 20
+
+
+def shift_rows(read_row, shifted, rows, side):
+    def body(r, carry):
+        line = read_row(r)
+        for b in range(7):
+            shifted[b, r] = line[b : b + side].reshape(side // 8, 8, 128)
+        return carry
+
+    lax.fori_loop(0, rows, body, 0, unroll=2)
+
+
+def conv_kernel(group, flip, map_ref, tap_ref, out_ref, shifted, taps):
+    rows, side = out_ref.shape[1], out_ref.shape[2]
+    for k in range(49):
+        tap = tap_ref[48 - k if flip else k].reshape(1, 128)
+        taps[k] = jnp.broadcast_to(tap, (8, 128))
+    shift_rows(lambda r: map_ref[0, r].astype(jnp.float32), shifted, rows + 6, side)
+
+    def body(g, carry):
+        first = g * group
+        sums = [jnp.zeros((side // 8, 8, 128), jnp.float32) for _ in range(group)]
+        for b in range(7):
+            for r in range(group + 6):
+                line = shifted[b, first + r]
+                for k in range(group):
+                    if 0 <= r - k < 7:
+                        sums[k] = sums[k] + taps[(r - k) * 7 + b][None] * line
+        for k in range(group):
+            out_ref[0, first + k] = sums[k].reshape(side, 128)
+        return carry
+
+    lax.fori_loop(0, rows // group, body, 0)
+
+
+def depthwise_seven(padded, tap_weights, flip):
+    slots, rows, cols, channels = padded.shape
+    side = rows - 6
+    return pl.pallas_call(
+        partial(conv_kernel, 4, flip),
+        grid=(slots, channels // 128),
+        in_specs=[
+            pl.BlockSpec((1, rows, cols, 128), lambda s, c: (s, 0, 0, c)),
+            pl.BlockSpec((49, 128), lambda s, c: (0, c)),
+        ],
+        out_specs=pl.BlockSpec((1, side, side, 128), lambda s, c: (s, 0, 0, c)),
+        out_shape=jax.ShapeDtypeStruct((slots, side, side, channels), jnp.float32),
+        scratch_shapes=[
+            pltpu.VMEM((7, rows, side // 8, 8, 128), jnp.float32),
+            pltpu.VMEM((49, 8, 128), jnp.float32),
+        ],
+        cost_estimate=pl.CostEstimate(
+            flops=98 * slots * side * side * channels,
+            bytes_accessed=8 * slots * side * side * channels,
+            transcendentals=0,
+        ),
+        compiler_params=pltpu.CompilerParams(vmem_limit_bytes=VMEM_LIMIT),
+        name="depthwise_seven",
+    )(padded, tap_weights)
+
+
+def tap_grad_kernel(group, map_ref, grad_ref, out_ref, shifted):
+    rows, side = grad_ref.shape[1], grad_ref.shape[2]
+    shift_rows(lambda r: map_ref[0, r].astype(jnp.float32), shifted, rows + 6, side)
+
+    @pl.when(pl.program_id(1) == 0)
+    def _():
+        out_ref[...] = jnp.zeros_like(out_ref)
+
+    for columns in ((0, 1, 2, 3), (4, 5, 6)):
+
+        def body(g, sums):
+            sums = [list(part) for part in sums]
+            first = g * group
+            lines = [
+                grad_ref[0, first + k].astype(jnp.float32).reshape(side // 8, 8, 128)
+                for k in range(group)
+            ]
+            for n, b in enumerate(columns):
+                for r in range(group + 6):
+                    line = shifted[b, first + r]
+                    for k in range(group):
+                        if 0 <= r - k < 7:
+                            sums[r - k][n] = sums[r - k][n] + jnp.sum(line * lines[k], axis=0)
+            return tuple(tuple(part) for part in sums)
+
+        zero = jnp.zeros((8, 128), jnp.float32)
+        sums = lax.fori_loop(
+            0, rows // group, body, tuple(tuple(zero for _ in columns) for _ in range(7))
+        )
+        for a in range(7):
+            for n, b in enumerate(columns):
+                row = pl.ds(a * 7 + b, 1)
+                out_ref[row, :] = out_ref[row, :] + jnp.sum(sums[a][n], axis=0, keepdims=True)
+
+
+def tap_grad_seven(padded, grad):
+    slots, rows, cols, channels = padded.shape
+    side = rows - 6
+    return pl.pallas_call(
+        partial(tap_grad_kernel, 4),
+        grid=(channels // 128, slots),
+        in_specs=[
+            pl.BlockSpec((1, rows, cols, 128), lambda c, s: (s, 0, 0, c)),
+            pl.BlockSpec((1, side, side, 128), lambda c, s: (s, 0, 0, c)),
+        ],
+        out_specs=pl.BlockSpec((49, 128), lambda c, s: (0, c)),
+        out_shape=jax.ShapeDtypeStruct((49, channels), jnp.float32),
+        scratch_shapes=[pltpu.VMEM((7, rows, side // 8, 8, 128), jnp.float32)],
+        cost_estimate=pl.CostEstimate(
+            flops=98 * slots * side * side * channels,
+            bytes_accessed=8 * slots * side * side * channels,
+            transcendentals=0,
+        ),
+        compiler_params=pltpu.CompilerParams(vmem_limit_bytes=VMEM_LIMIT),
+        name="tap_grad_seven",
+    )(padded, grad)
+
+
+PIECE_BYTES = 2_000_000
+COPIES = 8
+SMALL_ROWS = 512
+
+
+def plan_pieces(shapes):
+    pieces = []
+    for g, (height, width) in enumerate(shapes):
+        rows = height // 8
+        count = max(1, round(height * width * 2 / PIECE_BYTES))
+        while rows % (count * 32):
+            count -= 1
+        for p in range(count):
+            pieces.append((g, p * (rows // count), rows // count))
+    return pieces
+
+
+def wide_sum(one, two):
+    return one.astype(jnp.float32) + two.astype(jnp.float32)
+
+
+def low_sum(one, two):
+    return wide_sum(one, two).astype(jnp.bfloat16)
+
+
+def row_loop(first, rows, step):
+    def body(q, carry):
+        step(pl.ds(pl.multiple_of(first + q * 16, 16), 16))
+        return carry
+
+    lax.fori_loop(0, rows // 16, body, 0)
+
+
+def reduce_kernel(pieces, shapes, *refs):
+    matrices = len(shapes)
+    count = len(pieces)
+    grads, small = refs[:matrices], refs[matrices]
+    outs, small_out = refs[matrices + 1 : 2 * matrices + 1], refs[2 * matrices + 1]
+    scratch = refs[2 * matrices + 2 :]
+    own, half, quarter, eighth, pair, last = (
+        scratch[k * count : (k + 1) * count] for k in range(6)
+    )
+    small_work, small_in, send_sem, recv_sem, own_sem, small_send, small_recv = scratch[6 * count :]
+    img = lax.axis_index("img")
+    tile = lax.axis_index("tile")
+    core, x, y = img % 2, (img // 2) % 2, img // 4
+    low, high = tile % 2, tile // 2
+    to_core = (img + 1 - 2 * core, tile)
+    to_x = (img + 2 - 4 * x, tile)
+    to_y = (img + 4 - 8 * y, tile)
+    to_low = (img, tile + 1 - 2 * low)
+    to_high = (img, tile + 2 - 4 * high)
+    barrier = pltpu.get_barrier_semaphore()
+    for partner in (to_core, to_x, to_y, to_low, to_high):
+        pl.semaphore_signal(barrier, inc=1, device_id=partner, device_id_type=MESH)
+    pl.semaphore_wait(barrier, 5)
+    started = []
+    waiting = {}
+
+    def send(source, target, sems, index, partner):
+        copy = pltpu.make_async_remote_copy(
+            src_ref=source,
+            dst_ref=target,
+            send_sem=sems[0].at[index],
+            recv_sem=sems[1].at[index],
+            device_id=partner,
+            device_id_type=MESH,
+        )
+        copy.start()
+        started.append(copy)
+        return copy
+
+    def send_piece(i, k, source, target, partner):
+        return send(source, target, (send_sem, recv_sem), i * COPIES + k, partner)
+
+    def over_core(i):
+        g, first, rows = pieces[i]
+        part = pl.ds(first, rows)
+        copy = send_piece(i, 0, grads[g].at[:, :, 1 - core, part, :], half[i], to_core)
+        local_copy = pltpu.make_async_copy(
+            grads[g].at[:, :, core, part, :], own[i], own_sem.at[i]
+        )
+        local_copy.start()
+        waiting[i] = (copy, local_copy)
+
+    def over_first(i):
+        g, first, rows = pieces[i]
+        cut = rows // 2
+        copy, local_copy = waiting[i]
+        copy.wait_recv()
+        local_copy.wait()
+        for a in range(2):
+            for b in range(2):
+
+                def step(s, a=a, b=b):
+                    half[i][a, b, s, :] = low_sum(half[i][a, b, s, :], own[i][a, b, s, :])
+
+                row_loop(0, rows, step)
+        top, bottom = pl.ds(0, cut), pl.ds(cut, cut)
+        waiting[i] = (
+            send_piece(i, 1, half[i].at[:, 1 - x, top, :], quarter[i].at[:, top, :], to_x),
+            send_piece(i, 2, half[i].at[1 - y, :, bottom, :], quarter[i].at[:, bottom, :], to_y),
+        )
+
+    def over_second(i):
+        g, first, rows = pieces[i]
+        cut = rows // 2
+        for copy in waiting[i]:
+            copy.wait_recv()
+        for a in range(2):
+
+            def step_top(s, a=a):
+                quarter[i][a, s, :] = low_sum(quarter[i][a, s, :], half[i][a, x, s, :])
+
+            def step_bottom(s, a=a):
+                quarter[i][a, s, :] = low_sum(quarter[i][a, s, :], half[i][y, a, s, :])
+
+            row_loop(0, cut, step_top)
+            row_loop(cut, cut, step_bottom)
+        top, bottom = pl.ds(0, cut), pl.ds(cut, cut)
+        waiting[i] = (
+            send_piece(i, 3, quarter[i].at[1 - y, top, :], eighth[i].at[top, :], to_y),
+            send_piece(i, 4, quarter[i].at[1 - x, bottom, :], eighth[i].at[bottom, :], to_x),
+        )
+
+    def lanes(start, size):
+        return pl.ds(pl.multiple_of(start, 128), size)
+
+    def over_third(i):
+        g, first, rows = pieces[i]
+        cut = rows // 2
+        width = shapes[g][1] // 4
+        for copy in waiting[i]:
+            copy.wait_recv()
+
+        def step_top(s):
+            eighth[i][s, :] = low_sum(eighth[i][s, :], quarter[i][y, s, :])
+
+        def step_bottom(s):
+            eighth[i][s, :] = low_sum(eighth[i][s, :], quarter[i][x, s, :])
+
+        row_loop(0, cut, step_top)
+        row_loop(cut, cut, step_bottom)
+        if width % 128 == 0:
+            waiting[i] = tuple(
+                send_piece(
+                    i,
+                    5 + q,
+                    eighth[i].at[:, lanes((2 * q + 1 - low) * width, width)],
+                    pair[i].at[:, pl.ds(q * width, width)],
+                    to_low,
+                )
+                for q in range(2)
+            )
+        else:
+            side = eighth[i].at[:, lanes((1 - high) * 2 * width, 2 * width)]
+            waiting[i] = (send_piece(i, 5, side, pair[i], to_high),)
+
+    def over_fourth(i):
+        g, first, rows = pieces[i]
+        width = shapes[g][1] // 4
+        for copy in waiting[i]:
+            copy.wait_recv()
+        if width % 128 == 0:
+
+            def step(s):
+                for q in range(2):
+                    at = slice(q * width, (q + 1) * width)
+                    kept = eighth[i][s, lanes((2 * q + low) * width, width)]
+                    pair[i][s, at] = low_sum(pair[i][s, at], kept)
+
+            row_loop(0, rows, step)
+            side = pair[i].at[:, lanes((1 - high) * width, width)]
+            waiting[i] = (send_piece(i, 7, side, last[i], to_high),)
+        else:
+
+            def step(s):
+                kept = eighth[i][s, lanes(high * 2 * width, 2 * width)]
+                pair[i][s, :] = low_sum(pair[i][s, :], kept)
+
+            row_loop(0, rows, step)
+            waiting[i] = (send_piece(i, 7, pair[i], last[i], to_low),)
+
+    def finish(i):
+        g, first, rows = pieces[i]
+        width = shapes[g][1] // 4
+        for copy in waiting[i]:
+            copy.wait_recv()
+
+        def step(s):
+            at = pl.ds(pl.multiple_of(s.start + first, 16), 16)
+            if width % 128 == 0:
+                kept = pair[i][s, lanes(high * width, width)]
+                outs[g][at, :] = wide_sum(last[i][s, :], kept)
+            else:
+                both = wide_sum(last[i][s, :], pair[i][s, :])
+                outs[g][at, :] = jnp.where(low == 0, both[:, :width], both[:, width:])
+
+        row_loop(0, rows, step)
+
+    halvings = ((to_core, core), (to_x, x), (to_y, y), (to_low, low), (to_high, high))
+    total = small.shape[0]
+    small_sems = (small_send, small_recv)
+    place = {"start": 0, "size": total}
+
+    def rows_at(start, size):
+        return pl.ds(pl.multiple_of(start, 8), size)
+
+    def small_step(k):
+        if k == 0:
+            small_work[...] = small[...]
+        else:
+            waiting["small"].wait_recv()
+        if 1 <= k <= 5:
+            size = place["size"]
+            at = rows_at(place["start"], size)
+            summed = small_work[at, :] + small_in[pl.ds(total - 2 * size, size), :]
+            if k < 5:
+                small_work[at, :] = summed
+            else:
+                small_out[at, :] = summed
+        if k < 5:
+            partner, bit = halvings[k]
+            size = place["size"] // 2
+            give = rows_at(place["start"] + (1 - bit) * size, size)
+            waiting["small"] = send(
+                small_work.at[give, :],
+                small_in.at[pl.ds(total - 2 * size, size), :],
+                small_sems,
+                k,
+                partner,
+            )
+            place["start"] = place["start"] + bit * size
+            place["size"] = size
+        elif k < 10:
+            partner, bit = halvings[9 - k]
+            if k > 5:
+                before = halvings[10 - k][1]
+                place["start"] = place["start"] - before * place["size"]
+                place["size"] = place["size"] * 2
+            mine = rows_at(place["start"], place["size"])
+            waiting["small"] = send(
+                small_out.at[mine, :], small_out.at[mine, :], small_sems, k, partner
+            )
+
+    stages = (over_core, over_first, over_second, over_third, over_fourth, finish)
+    for step in range(count + 10):
+        for k in range(len(stages) - 1, -1, -1):
+            i = step - 2 * k
+            if 0 <= i < count:
+                stages[k](i)
+        if step <= 10:
+            small_step(step)
+    for copy in started:
+        copy.wait_send()
+
+
+def reduce_matrices(grads, small):
+    shapes = [grad.shape for grad in grads]
+    pieces = plan_pieces(shapes)
+    count = len(pieces)
+    operands = [
+        grad.reshape(2, 2, 2, grad.shape[0] // 8, grad.shape[1]) for grad in grads
+    ]
+
+    def buffers(shape_of):
+        return [
+            pltpu.VMEM(shape_of(rows, shapes[g][1]), jnp.bfloat16) for g, _, rows in pieces
+        ]
+
+    scratch = buffers(lambda rows, width: (2, 2, rows, width))
+    scratch += buffers(lambda rows, width: (2, 2, rows, width))
+    scratch += buffers(lambda rows, width: (2, rows, width))
+    scratch += buffers(lambda rows, width: (rows, width))
+    scratch += buffers(lambda rows, width: (rows, width // 2))
+    scratch += buffers(
+        lambda rows, width: (rows, width // 4 if width % 512 == 0 else width // 2)
+    )
+    scratch += [
+        pltpu.VMEM(small.shape, jnp.float32),
+        pltpu.VMEM(small.shape, jnp.float32),
+        pltpu.SemaphoreType.DMA((count * COPIES,)),
+        pltpu.SemaphoreType.DMA((count * COPIES,)),
+        pltpu.SemaphoreType.DMA((count,)),
+        pltpu.SemaphoreType.DMA((10,)),
+        pltpu.SemaphoreType.DMA((10,)),
+    ]
+    in_vmem = pl.BlockSpec(memory_space=pltpu.VMEM)
+    results = pl.pallas_call(
+        partial(reduce_kernel, pieces, shapes),
+        in_specs=[pl.BlockSpec(memory_space=pl.ANY)] * len(grads) + [in_vmem],
+        out_specs=[in_vmem] * (len(grads) + 1),
+        out_shape=[
+            jax.ShapeDtypeStruct((height // 8, width // 4), jnp.float32)
+            for height, width in shapes
+        ]
+        + [jax.ShapeDtypeStruct(small.shape, jnp.float32)],
+        scratch_shapes=scratch,
+        compiler_params=pltpu.CompilerParams(
+            collective_id=0, has_side_effects=True, vmem_limit_bytes=VMEM_LIMIT
+        ),
+        name="reduce_matrices",
+    )(*operands, small)
+    return results[:-1], results[-1]
+
+
+def sum_everywhere(grads, smalls):
+    if lax.axis_size("img") == 8 and lax.axis_size("tile") == 4:
+        flat = jnp.concatenate([part.reshape(-1) for part in smalls])
+        flat = jnp.pad(flat, (0, SMALL_ROWS * 128 - flat.size)).reshape(SMALL_ROWS, 128)
+        sums, small = reduce_matrices(grads, flat)
+        flat = small.reshape(-1)
+        parts, first = [], 0
+        for part in smalls:
+            parts.append(flat[first : first + part.size].reshape(part.shape))
+            first += part.size
+        return sums, parts
+    sums = []
+    for grad in grads:
+        part = lax.psum_scatter(grad, "img", scatter_dimension=0, tiled=True)
+        part = lax.psum_scatter(part, "tile", scatter_dimension=1, tiled=True)
+        sums.append(part.astype(jnp.float32))
+    return sums, lax.psum(tuple(smalls), ("img", "tile"))
 
 
 def local(
@@ -195,18 +649,15 @@
     residual_one = tokens + project(mixed_low, w_out)
     normed_two, norm_two_pull = jax.vjp(layer_norm, residual_one, gain_mlp.astype(jnp.float32))
     normed_two_low = normed_two.astype(jnp.bfloat16)
-    acted, acted_pull = jax.vjp(gelu_exact, project(normed_two_low, w_up))
-    acted_low = acted.astype(jnp.bfloat16)
+    acted_low, acted_slope = gelu_pair(project(normed_two_low, w_up))
     residual_two = residual_one + project(acted_low, w_down)
     map_low = map_in[:, 0].reshape(slot_count, pix_side, pix_side, channels)
-    padded_map = add_rims(map_low, 3).astype(jnp.float32)
-    spread_map, spread_pull = jax.vjp(
-        partial(depthwise, radius=3, margin=0), padded_map, dw_large.astype(jnp.float32)
-    )
+    padded_map = add_rims(map_low, 3)
+    large_taps = dw_large.astype(jnp.float32)
+    spread_map = depthwise_seven(padded_map, large_taps, False)
     conv_norm, conv_norm_pull = jax.vjp(layer_norm, spread_map, gain_conv.astype(jnp.float32))
     conv_norm_low = conv_norm.astype(jnp.bfloat16)
-    wide_act, wide_pull = jax.vjp(gelu_exact, project(conv_norm_low, w_expand))
-    wide_low = wide_act.astype(jnp.bfloat16)
+    wide_low, wide_slope = gelu_pair(project(conv_norm_low, w_expand))
     map_after = map_low.astype(jnp.float32) + project(wide_low, w_shrink)
     pooled, pool_pull = jax.vjp(pool_pairs, map_after)
     pooled_low = pooled.astype(jnp.bfloat16)
@@ -237,14 +688,17 @@
     grad_map_after = map_cotangent + pool_pull(project_back(grad_adapted_low, w_adapt))[0]
     grad_conv_low = grad_map_after.astype(jnp.bfloat16)
     w_shrink_grad = outer_sum(wide_low, grad_conv_low)
-    grad_wide_low = wide_pull(project_back(grad_conv_low, w_shrink))[0].astype(jnp.bfloat16)
+    grad_wide_low = (project_back(grad_conv_low, w_shrink) * wide_slope).astype(jnp.bfloat16)
     w_expand_grad = outer_sum(conv_norm_low, grad_wide_low)
     grad_spread, gain_conv_grad = conv_norm_pull(project_back(grad_wide_low, w_expand))
-    grad_padded_map, dw_large_grad = spread_pull(grad_spread)
-    map_in_grad = (grad_map_after + return_rims(grad_padded_map, 3)).astype(jnp.bfloat16)
+    dw_large_grad = tap_grad_seven(padded_map, grad_spread)
+    padded_grad = add_rims(grad_spread.astype(jnp.bfloat16), 3)
+    map_in_grad = (grad_map_after + depthwise_seven(padded_grad, large_taps, True)).astype(
+        jnp.bfloat16
+    )
     grad_mlp_low = grad_residual_two.astype(jnp.bfloat16)
     w_down_grad = outer_sum(acted_low, grad_mlp_low)
-    grad_up_low = acted_pull(project_back(grad_mlp_low, w_down))[0].astype(jnp.bfloat16)
+    grad_up_low = (project_back(grad_mlp_low, w_down) * acted_slope).astype(jnp.bfloat16)
     w_up_grad = outer_sum(normed_two_low, grad_up_low)
     grad_norm_part, gain_mlp_grad = norm_two_pull(project_back(grad_up_low, w_up))
     grad_residual_one = grad_residual_two + grad_norm_part
@@ -309,47 +763,18 @@
     )
     grad_token_part, gain_attn_grad = norm_one_pull(grad_normed_one)
     vit_in_grad = (grad_residual_one + grad_token_part).astype(jnp.bfloat16)
-    by_group = (
-        lax.psum_scatter(w_query_grad, "img", scatter_dimension=0, tiled=True),
-        lax.psum_scatter(w_key_grad, "img", scatter_dimension=0, tiled=True),
-        lax.psum_scatter(w_value_grad, "img", scatter_dimension=0, tiled=True),
-        lax.psum_scatter(w_out_grad, "img", scatter_dimension=0, tiled=True),
-        lax.psum_scatter(w_up_grad, "img", scatter_dimension=0, tiled=True),
-        lax.psum_scatter(w_down_grad, "img", scatter_dimension=0, tiled=True),
-        lax.psum_scatter(w_expand_grad, "img", scatter_dimension=0, tiled=True),
-        lax.psum_scatter(w_shrink_grad, "img", scatter_dimension=0, tiled=True),
-        lax.psum_scatter(w_adapt_grad, "img", scatter_dimension=0, tiled=True),
-    )
-    matrix_sums = (
-        lax.psum_scatter(
-            by_group[0].astype(jnp.bfloat16), "tile", scatter_dimension=1, tiled=True
-        ).astype(jnp.float32),
-        lax.psum_scatter(
-            by_group[1].astype(jnp.bfloat16), "tile", scatter_dimension=1, tiled=True
-        ).astype(jnp.float32),
-        lax.psum_scatter(
-            by_group[2].astype(jnp.bfloat16), "tile", scatter_dimension=1, tiled=True
-        ).astype(jnp.float32),
-        lax.psum_scatter(
-            by_group[3].astype(jnp.bfloat16), "tile", scatter_dimension=1, tiled=True
-        ).astype(jnp.float32),
-        lax.psum_scatter(
-            by_group[4].astype(jnp.bfloat16), "tile", scatter_dimension=1, tiled=True
-        ).astype(jnp.float32),
-        lax.psum_scatter(
-            by_group[5].astype(jnp.bfloat16), "tile", scatter_dimension=1, tiled=True
-        ).astype(jnp.float32),
-        lax.psum_scatter(
-            by_group[6].astype(jnp.bfloat16), "tile", scatter_dimension=1, tiled=True
-        ).astype(jnp.float32),
-        lax.psum_scatter(
-            by_group[7].astype(jnp.bfloat16), "tile", scatter_dimension=1, tiled=True
-        ).astype(jnp.float32),
-        lax.psum_scatter(
-            by_group[8].astype(jnp.bfloat16), "tile", scatter_dimension=1, tiled=True
-        ).astype(jnp.float32),
-    )
-    small_sums = lax.psum(
+    matrix_sums, small_sums = sum_everywhere(
+        (
+            w_up_grad,
+            w_down_grad,
+            w_adapt_grad,
+            w_expand_grad,
+            w_shrink_grad,
+            w_query_grad,
+            w_key_grad,
+            w_value_grad,
+            w_out_grad,
+        ),
         (
             gain_attn_grad,
             gain_mlp_grad,
@@ -359,7 +784,17 @@
             gate_low_grad,
             gate_high_grad,
         ),
-        ("img", "tile"),
+    )
+    matrix_sums = (
+        matrix_sums[5],
+        matrix_sums[6],
+        matrix_sums[7],
+        matrix_sums[8],
+        matrix_sums[0],
+        matrix_sums[1],
+        matrix_sums[3],
+        matrix_sums[4],
+        matrix_sums[2],
     )
     vit_result = (vit_after * live_mask).astype(jnp.bfloat16)[:, None]
     map_result = (

time: 1300 us -> 652 us (0.50)
  waiting for transfers between devices: 605 us -> 41.9 us
  Pallas kernels: 0 us -> 230 us
  matrix products: 403 us -> 189 us
  other arithmetic: 124 us -> 74.7 us
  blocking collectives: 42.7 us -> 0 us
    reduce_scatter x12 -> x0, waiting for transfers between devices: 401 us -> none  [the longest x1 86.8 us: local(): lax.psum_scatter(w_shrink_grad, 'img', scatter_dimension=0, tiled=True)]
    pallas_call x0 -> x4, Pallas kernels: none -> 230 us  [the longest x1 156 us: reduce_matrices(): pl.pallas_call(partial(reduce_kernel, pieces, shapes), in_specs=[pl.Block...]
    conv_general_dilated x6 -> x3, matrix products: 213 us -> 10.5 us  [depthwise(): lax.conv_general_dilated(field_map, kernel, (1, 1), ((margin, margin), (m...]
    psum x1 -> x0, waiting for transfers between devices: 126 us -> none  [local(): lax.psum((gain_attn_grad, gain_mlp_grad, gain_conv_grad, dw_large_grad, d...]
    psum x1 -> x0, blocking collectives: 42.7 us -> none  [local(): lax.psum((gain_attn_grad, gain_mlp_grad, gain_conv_grad, dw_large_grad, d...]
    convert_element_type x18 -> x3, other arithmetic: 36.6 us -> 14 us  [the longest x1 10.3 us: local(): (grad_map_after + depthwise_seven(padded_grad, large_taps, True)).astype(...]
    ppermute x8, waiting for transfers between devices: 63.8 us -> 41.8 us  [swapped(): lax.ppermute(array, axis, [(i, i ^ 1 << bit) for i in range(lax.axis_size...]
    reduce_scatter x1, waiting for transfers between devices: 13.5 us -> 0.02 us  [local(): lax.psum_scatter(grad_key_term.astype(jnp.bfloat16), 'tile', scatter_dime...]
  transfers between devices with their start and end apart: 31 -> 12, of which waited for: 17 -> 5; matrix products, arithmetic and copies ran while one was open for 42% -> 37% of each run, Pallas kernels for 0% -> 12%
where the time goes in v1:
time: 652 us; the launch traced here: 647 us
  Pallas kernels  230 us (35%)
  matrix products  189 us (29%)
  local copies, waits for them, and re-layouts  77.5 us (12%)
  other arithmetic  74.7 us (11%)
  waiting for transfers between devices  41.9 us (6%)
  starting transfers between devices  16.5 us (3%)
  between operations  16.3 us (2%)
    pallas_call x1, Pallas kernels, reduce_matrices(): pl.pallas_call(partial(reduce_kernel, pieces, shapes), in_specs=[pl.Block...  156 us
    dot_general x9, matrix products, outer_sum(): lax.dot_general(flat_left, flat_right, (((0,), (0,)), ((), ())), preferre...  54.5 us
    dot_general x9, matrix products, project_back(): jnp.einsum('...j,ij->...i', left_side, right_side, preferred_element_type...  54.1 us
    pallas_call x2, Pallas kernels, depthwise_seven(): pl.pallas_call(partial(conv_kernel, 4, flip), grid=(slots, channels // 12...  50.9 us
    dot_general x9, matrix products, project(): jnp.einsum('...i,ij->...j', left_side, right_side, preferred_element_type...  46.5 us
    ppermute x8, waiting for transfers between devices, swapped(): lax.ppermute(array, axis, [(i, i ^ 1 << bit) for i in range(lax.axis_size...  41.8 us
    unnamed x261, local copies, waits for them, and re-layouts  25.4 us
    pallas_call x1, Pallas kernels, tap_grad_seven(): pl.pallas_call(partial(tap_grad_kernel, 4), grid=(channels // 128, slots)...  23.5 us
  transfers between devices with their start and end apart: 12, of which 5 were waited for; matrix products, arithmetic and copies ran while one was open for 37% of the time, Pallas kernels for 12%

profile of v1, /device:TPU:0, one launch (start us, length us, event | category | flops | bytes accessed | tf_op | source)
XLA Modules:
  0.0 646.6 jit_solution(5775756759415683151)
XLA Ops:
  11.1 2.7 convolution_convert_fusion.1
  15.6 3.1 collective-permute-start
  18.7 11.7 %collective-permute-done = bf16[2,24,3,1024]{3,2,1,0:T(4,128)(2,1)S(1)} collective-permute-done((bf16[2,24,3,1024]{3,2,1,0:T(4,128)(2,1)S(1)}, bf16[2,24,3,1024]{3,2,1,0:T(4,128)(2,1)S(1)}, u32[]{:S(2)}, u32[]{:S(2)}) %collective-permute-start) | collective-permute-done | bytes 294944 | tf_op jit(solution)/shard_map/ppermute | solution.py:19
  31.3 3.9 fusion.43
  37.6 7.7 %collective-permute-start.1 = (bf16[2,3,30,1024]{3,2,1,0:T(8,128)(2,1)}, bf16[2,3,30,1024]{3,2,1,0:T(8,128)(2,1)}, u32[]{:S(2)}, u32[]{:S(2)}) collective-permute-start(bf16[2,3,30,1024]{3,2,1,0:T(8,128)(2,1)} %slice_select_fusion.2), channel_id=1, source_target_pairs={{0,2},{1,3},{2,0},{3,1},{4,6},{5,7},{6,4},{7,5},{8,10},{9,11},{10,... | collective-permute-start | bytes 1105928 | tf_op jit(solution)/shard_map/ppermute | solution.py:19
  49.0 24.8 %collective-permute-done.1 = bf16[2,3,30,1024]{3,2,1,0:T(8,128)(2,1)} collective-permute-done((bf16[2,3,30,1024]{3,2,1,0:T(8,128)(2,1)}, bf16[2,3,30,1024]{3,2,1,0:T(8,128)(2,1)}, u32[]{:S(2)}, u32[]{:S(2)}) %collective-permute-start.1) | collective-permute-done | bytes 368672 | tf_op jit(solution)/shard_map/ppermute | solution.py:19
  74.6 3.3 fusion.34.map_ref
  77.9 25.3 %depthwise_seven.2 = f32[2,24,24,1024]{3,2,1,0:T(8,128)} custom-call(bf16[2,30,30,1024]{3,2,1,0:T(8,128)(2,1)} %fusion.34.map_ref, f32[49,1024]{1,0:T(8,128)} %convert_element_type.262.tap_ref), custom_call_target="tpu_custom_call" | custom-call | flops 115605504 | bytes 9437184 | tf_op jit(solution)/shard_map/depthwise_seven/pallas_call | solution.py:186
  103.2 2.6 reduce_sum.223
  105.9 3.1 multiply_reduce_fusion.4
  109.7 18.0 %multiply_convert_fusion.1 = (bf16[2,24,24,4096]{3,2,1,0:T(8,128)(2,1)S(1)}, f32[2,24,24,4096]{3,2,1,0:T(8,128)}) fusion(bf16[1024,4096]{1,0:T(8,128)(2,1)} %param.32, f32[2,24,24,1024]{3,2,1,0:T(8,128)S(1)} %copy-done.3, f32[1024]{0:T(1024)S(1)} %convert_element_type.263, f32[2,24,24]{2,1,0:T(8,128)S(1)} %fusion.116, ...), kind=kOutput, calls=%fused_computation.7 | convolution fusion | flops 9691987968 | bytes 41432064 | tf_op jit(solution)/shard_map/...i,ij->...j/dot_general | solution.py:69
  127.7 3.6 copy-done.110
  131.3 11.8 %convert_add_fusion = f32[2,24,24,1024]{3,2,1,0:T(8,128)} fusion(bf16[2,24,24,1024]{3,2,1,0:T(8,128)(2,1)S(1)} %bitcast.294, bf16[2,24,24,4096]{3,2,1,0:T(8,128)(2,1)S(1)} %get-tuple-element.153, bf16[4096,1024]{1,0:T(8,128)(2,1)S(1)} %bitcast.310), kind=kOutput, calls=%fused_computation.50 | convolution fusion | flops 9666035712 | bytes 24903680 | tf_op jit(solution)/shard_map/...i,ij->...j/dot_general | solution.py:69
  143.1 7.0 %reshape.329 = f32[2,12,2,12,2,1024]{5,4,3,2,1,0:T(2,128)} reshape(f32[2,24,24,1024]{3,2,1,0:T(8,128)} %convert_add_fusion) | data formatting | bytes 9437184 | tf_op jit(solution)/shard_map/jvp()/reshape | solution.py:56
  150.1 7.3 %reduce_sum.225 = f32[2,12,12,1024]{3,2,1,0:T(8,128)} reduce(f32[2,12,2,12,2,1024]{5,4,3,2,1,0:T(2,128)} %reshape.329, f32[]{:T(128)} %constant.20.clone.1), dimensions={2,4}, to_apply=%region_9.10 | reduce | flops 884736 | bytes 5898244 | tf_op jit(solution)/shard_map/jvp()/reduce_sum | solution.py:55
  160.6 3.6 collective-permute-done.2
  171.9 3.1 multiply_reduce_fusion.9
  177.6 2.7 copy.137
  180.4 2.6 multiply_reduce_fusion.1
  187.7 4.3 copy.135
  192.1 6.4 fusion.60
  199.5 3.7 multiply_convert_fusion.6
  203.3 4.7 multiply_reduce_fusion.11
  208.6 6.1 fusion.31
  223.9 7.4 %multiply_reduce_fusion = (f32[2,12,144]{2,1,0:T(8,128)S(1)}, f32[2,12,144,576]{3,2,1,0:T(8,128)S(1)}) fusion(f32[2,12,144,576]{3,2,1,0:T(8,128)} %copy-done.2, f32[2,12,144]{2,1,0:T(8,128)} %log_add_fusion, bf16[2,144,12,64]{1,3,2,0:T(8,128)(2,1)} %bitcast.286, bf16[2,576,12,64]{1,3,2,0:T(8,128)(2,1)} %bitcast.283), kind=kOutput, calls=%fused_computation.14 | convolution fusion | flops 262763136 | bytes 18164736 | tf_op jit(solution)/shard_map/sqhd,skhd->shqk/dot_general | solution.py:712
  235.8 2.8 multiply_convert_fusion.7
  239.5 4.0 copy.148
  247.4 3.3 fusion.135
  250.8 2.5 collective-permute-start.4
  255.3 4.5 bitcast_convert_fusion.2
  259.8 4.6 bitcast_convert_fusion.3
  266.8 4.1 convolution_reduce_fusion
  276.2 2.8 copy.149
  285.3 4.4 broadcast_in_dim.68
  289.7 6.9 %reshape.334 = f32[2,24,24,1024]{3,2,1,0:T(8,128)} reshape(f32[2,12,2,12,2,1024]{5,4,3,2,1,0:T(2,128)} %broadcast_in_dim.68) | data formatting | bytes 9437184 | tf_op jit(solution)/shard_map/transpose(jvp())/reshape | solution.py:56
  296.6 4.2 fusion.47
  300.9 17.6 %bitcast_convert_fusion = bf16[4096,1024]{1,0:T(8,128)(2,1)} fusion(bf16[2,24,24,4096]{3,2,1,0:T(8,128)(2,1)} %copy-done.110, bf16[2,24,24,1024]{3,2,1,0:T(8,128)(2,1)S(1)} %fusion.47), kind=kOutput, calls=%fused_computation.9 | convolution fusion | flops 9667870720 | bytes 20185088 | tf_op jit(solution)/shard_map/dot_general | solution.py:79
  318.5 19.6 %multiply_convert_fusion = bf16[2,24,24,4096]{3,2,1,0:T(8,128)(2,1)} fusion(bf16[2,24,24,1024]{3,2,1,0:T(8,128)(2,1)S(1)} %fusion.47, f32[2,24,24,4096]{3,2,1,0:T(8,128)} %get-tuple-element.154, bf16[4096,1024]{1,0:T(8,128)(2,1)S(1)} %bitcast.312), kind=kOutput, calls=%fused_computation.6 | convolution fusion | flops 9720299520 | bytes 39059456 | tf_op jit(solution)/shard_map/...j,ij->...i/dot_general | solution.py:73
  338.1 16.6 %multiply_reduce_fusion.3 = (f32[2,24,24]{2,1,0:T(8,128)S(1)}, f32[2,24,24,1024]{3,2,1,0:T(8,128)}) fusion(f32[2,24,24,1024]{3,2,1,0:T(8,128)S(1)} %copy-done.4, f32[1024]{0:T(1024)S(1)} %copy-done.76, f32[2,24,24]{2,1,0:T(8,128)S(1)} %copy-done.54, bf16[2,24,24,4096]{3,2,1,0:T(8,128)(2,1)} %multiply_convert_fusion, bf16[1024,4096]{1,0:T(8,128)(2,1)} %param.32), kind=kOutput, calls=%fused_computation.46 | convolution fusion | flops 9668393984 | bytes 27276288 | tf_op jit(solution)/shard_map/...j,ij->...i/dot_general | solution.py:73
  354.8 4.2 multiply_reduce_fusion.2
  359.0 3.1 fusion.132
  363.4 17.7 %bitcast_convert_fusion.1 = bf16[1024,4096]{1,0:T(8,128)(2,1)} fusion(bf16[2,24,24,4096]{3,2,1,0:T(8,128)(2,1)} %multiply_convert_fusion, f32[2,24,24,1024]{3,2,1,0:T(8,128)S(1)} %copy-done.4, f32[1024]{0:T(1024)S(1)} %copy-done.76, f32[2,24,24]{2,1,0:T(8,128)S(1)} %copy-done.60, f32[2,24,24]{2,1,0:T(8,128)S(1)} %copy-done.54), kind=kOutput, calls=%fused_computation.10 | convolution fusion | flops 9672589312 | bytes 22557696 | tf_op jit(solution)/shard_map/dot_general | solution.py:79
  387.5 23.5 %tap_grad_seven.1 = f32[49,1024]{1,0:T(8,128)} custom-call(bf16[2,30,30,1024]{3,2,1,0:T(8,128)(2,1)} %fusion.34.map_ref, f32[2,24,24,1024]{3,2,1,0:T(8,128)} %get-tuple-element.129.grad_ref), custom_call_target="tpu_custom_call" | custom-call | flops 115605504 | bytes 9437184 | tf_op jit(solution)/shard_map/tap_grad_seven/pallas_call | solution.py:247
  412.1 3.8 fusion.35.map_ref
  415.8 25.5 %depthwise_seven.3 = f32[2,24,24,1024]{3,2,1,0:T(8,128)} custom-call(bf16[2,30,30,1024]{3,2,1,0:T(8,128)(2,1)} %fusion.35.map_ref, f32[49,1024]{1,0:T(8,128)} %convert_element_type.262.tap_ref), custom_call_target="tpu_custom_call" | custom-call | flops 115605504 | bytes 9437184 | tf_op jit(solution)/shard_map/depthwise_seven/pallas_call | solution.py:186
  441.4 10.3 %add_convert_fusion = (bf16[2,24,24,1024]{3,2,1,0:T(8,128)(2,1)}, bf16[2,24,24,1024]{3,2,1,0:T(8,128)(2,1)}) fusion(f32[2,24,24,1024]{3,2,1,0:T(8,128)} %depthwise_seven.3, f32[2,24,24,1024]{3,2,1,0:T(8,128)} %reshape.334, bf16[2,24,24,1024]{3,2,1,0:T(8,128)(2,1)} %bitcast.279, f32[2]{0:T(128)S(1)} %copy-done.96, f32[2,24,24,1024]{3,2,1,0:T(8,128)} %convert_add_fusion), kind=kLoop, calls=%fused_computation.45 | loop fusion | flops 8257536 | bytes 21233672 | tf_op jit(solution)/shard_map/convert_element_type | solution.py:696
  451.8 2.5 convolution_add_fusion.1
  462.8 156.0 %reduce_matrices.1 = (f32[96,768]{1,0:T(8,128)}, f32[384,192]{1,0:T(8,128)}, f32[128,192]{1,0:T(8,128)}, f32[128,1024]{1,0:T(8,128)}, f32[512,256]{1,0:T(8,128)}...) custom-call(bf16[2,2,2,96,3072]{4,3,2,1,0:T(8,128)(2,1)} %bitcast.29, ...), custom_call_target="tpu_custom_call" | custom-call | tf_op jit(solution)/shard_map/reduce_matrices/pallas_call | solution.py:555
  (381 shorter events, 105.2 us)
Async XLA Ops:
  7.2 150.2 %copy-start = (bf16[1024,768]{1,0:T(8,128)(2,1)S(1)}, bf16[1024,768]{1,0:T(8,128)(2,1)}, u32[]{:S(2)}) copy-start(bf16[1024,768]{1,0:T(8,128)(2,1)} %param.34) | copy-start | bytes 4718596
  7.2 170.4 %all-gather.5.cloned.1.call-start = ((), (), s32[]{:S(2)}) async-start(), calls=%async_computation.3 | async-start | bytes 2211840 | tf_op jit(solution)/shard_map/all_gather | solution.py:141
  8.5 39.1 %copy-start.71 = (f32[2,144]{1,0:T(2,128)}, f32[2,144]{1,0:T(2,128)S(1)}, u32[]{:S(2)}) copy-start(f32[2,144]{1,0:T(2,128)S(1)} %broadcast_multiply_fusion.2) | copy-start | bytes 3460
  10.4 37.2 %copy-start.84 = (f32[2,144]{1,0:T(2,128)}, f32[2,144]{1,0:T(2,128)S(1)}, u32[]{:S(2)}) copy-start(f32[2,144]{1,0:T(2,128)S(1)} %fusion.119) | copy-start | bytes 3460
  11.1 36.5 %copy-start.68 = (f32[768]{0:T(1024)}, f32[768]{0:T(1024)S(1)}, u32[]{:S(2)}) copy-start(f32[768]{0:T(1024)S(1)} %convert_element_type.248) | copy-start | bytes 9220
  13.9 173.9 %all-gather.3.cloned.1.call-start = ((), (), s32[]{:S(2)}) async-start(), calls=%async_computation.2 | async-start | bytes 2211840 | tf_op jit(solution)/shard_map/all_gather | solution.py:142
  15.6 14.8 %collective-permute-start = (bf16[2,24,3,1024]{3,2,1,0:T(4,128)(2,1)S(1)}, bf16[2,24,3,1024]{3,2,1,0:T(4,128)(2,1)S(1)}, u32[]{:S(2)}, u32[]{:S(2)}) collective-permute-start(bf16[2,24,3,1024]{3,2,1,0:T(4,128)(2,1)S(1)} %slice_select_fusion.3), channel_id=1, source_target_pairs={{0,1},{1,0},{2,3},{3,2},{4,5},{5,4},{6,7},{7,6},{8,9},{9,8},{10,11... | collective-permute-start | bytes 884744 | tf_op jit(solution)/shard_map/ppermute | solution.py:19
  18.7 26.6 %copy-start.9 = (bf16[2,1,144,768]{3,2,1,0:T(8,128)(2,1)S(1)}, bf16[2,1,144,768]{3,2,1,0:T(8,128)(2,1)}, u32[]{:S(2)}) copy-start(bf16[2,1,144,768]{3,2,1,0:T(8,128)(2,1)} %param.21) | copy-start | bytes 1327108
  18.7 26.6 %copy-start.41 = (bf16[768,768]{1,0:T(8,128)(2,1)S(1)}, bf16[768,768]{1,0:T(8,128)(2,1)}, u32[]{:S(2)}) copy-start(bf16[768,768]{1,0:T(8,128)(2,1)} %param.28) | copy-start | bytes 3538948
  31.3 15.6 %copy-start.63 = (bf16[49,1024]{1,0:T(8,128)(2,1)S(1)}, bf16[49,1024]{1,0:T(8,128)(2,1)}, u32[]{:S(2)}) copy-start(bf16[49,1024]{1,0:T(8,128)(2,1)} %param.38) | copy-start | bytes 301060
  31.3 16.3 %copy-start.102 = (bf16[1024]{0:T(1024)(128)(2,1)S(1)}, bf16[1024]{0:T(1024)(128)(2,1)}, u32[]{:S(2)}) copy-start(bf16[1024]{0:T(1024)(128)(2,1)} %param.37) | copy-start | bytes 6148
  31.3 16.3 %copy-start.39 = (bf16[768,768]{1,0:T(8,128)(2,1)S(1)}, bf16[768,768]{1,0:T(8,128)(2,1)}, u32[]{:S(2)}) copy-start(bf16[768,768]{1,0:T(8,128)(2,1)} %param.26) | copy-start | bytes 3538948
  37.6 36.2 %collective-permute-start.1 = (bf16[2,3,30,1024]{3,2,1,0:T(8,128)(2,1)}, bf16[2,3,30,1024]{3,2,1,0:T(8,128)(2,1)}, u32[]{:S(2)}, u32[]{:S(2)}) collective-permute-start(bf16[2,3,30,1024]{3,2,1,0:T(8,128)(2,1)} %slice_select_fusion.2), channel_id=1, source_target_pairs={{0,2},{1,3},{2,0},{3,1},{4,6},{5,7},{6,4},{7,5},{8,10},{9,11},{10,... | collective-permute-start | bytes 1105928 | tf_op jit(solution)/shard_map/ppermute | solution.py:19
  46.7 405.1 %reduce-scatter.3.cloned.1.call-start = ((), (), s32[]{:S(2)}) async-start(), calls=%async_computation.4 | async-start | bytes 2211840 | tf_op jit(solution)/shard_map/reduce_scatter | solution.py:747
  46.9 27.7 %copy-start.7 = (bf16[2,24,30,1024]{3,2,1,0:T(8,128)(2,1)S(1)}, bf16[2,24,30,1024]{3,2,1,0:T(8,128)(2,1)}, u32[]{:S(2)}) copy-start(bf16[2,24,30,1024]{3,2,1,0:T(8,128)(2,1)} %copy-done.6) | copy-start | bytes 8847364
  47.7 62.0 %copy-start.75 = (f32[1024]{0:T(1024)}, f32[1024]{0:T(1024)S(1)}, u32[]{:S(2)}) copy-start(f32[1024]{0:T(1024)S(1)} %convert_element_type.263) | copy-start | bytes 12292
  105.9 21.9 %copy-start.53 = (f32[2,24,24]{2,1,0:T(8,128)}, f32[2,24,24]{2,1,0:T(8,128)S(1)}, u32[]{:S(2)}) copy-start(f32[2,24,24]{2,1,0:T(8,128)S(1)} %broadcast_multiply_fusion) | copy-start | bytes 13828
  105.9 25.4 %slice-start.6 = ((s8[8388608]{0:T(1024)(128)(4,1)}), s8[4194304]{0:T(1024)(128)(4,1)S(1)}, s32[]{:S(2)}) async-start(s8[8388608]{0:T(1024)(128)(4,1)} %bitcast.309), calls=%async_computation.12 | async-start | bytes 8388608
  109.6 18.1 %copy-start.59 = (f32[2,24,24]{2,1,0:T(8,128)}, f32[2,24,24]{2,1,0:T(8,128)S(1)}, u32[]{:S(2)}) copy-start(f32[2,24,24]{2,1,0:T(8,128)S(1)} %fusion.116) | copy-start | bytes 13828
  109.6 21.7 %copy-start.20 = (bf16[2,1,576,1024]{3,2,1,0:T(8,128)(2,1)S(1)}, bf16[2,1,576,1024]{3,2,1,0:T(8,128)(2,1)}, u32[]{:S(2)}) copy-start(bf16[2,1,576,1024]{3,2,1,0:T(8,128)(2,1)} %param.22) | copy-start | bytes 7077892
  109.7 21.7 %slice-start.7 = ((s8[8388608]{0:T(1024)(128)(4,1)}), s8[4194304]{0:T(1024)(128)(4,1)S(1)}, s32[]{:S(2)}) async-start(s8[8388608]{0:T(1024)(128)(4,1)} %bitcast.309), calls=%async_computation.13 | async-start | bytes 8388608
  159.8 4.4 collective-permute-start.2
  165.6 5.1 collective-permute-start.3
  199.2 18.3 %copy-start.13 = (f32[2,144,768]{2,1,0:T(8,128)}, f32[2,144,768]{2,1,0:T(8,128)S(1)}, u32[]{:S(2)}) copy-start(f32[2,144,768]{2,1,0:T(8,128)S(1)} %get-tuple-element.150) | copy-start | bytes 2654212
  199.2 18.3 %copy-start.77 = (f32[2,144]{1,0:T(2,128)}, f32[2,144]{1,0:T(2,128)S(1)}, u32[]{:S(2)}) copy-start(f32[2,144]{1,0:T(2,128)S(1)} %broadcast_multiply_fusion.1) | copy-start | bytes 3460
  199.5 18.0 %copy-start.79 = (f32[2,144]{1,0:T(2,128)}, f32[2,144]{1,0:T(2,128)S(1)}, u32[]{:S(2)}) copy-start(f32[2,144]{1,0:T(2,128)S(1)} %fusion.120) | copy-start | bytes 3460
  203.3 11.4 %slice-start.10 = ((s8[4718592]{0:T(1024)(128)(4,1)}), s8[4194304]{0:T(1024)(128)(4,1)S(1)}, s32[]{:S(2)}) async-start(s8[4718592]{0:T(1024)(128)(4,1)} %bitcast.313), calls=%async_computation.16 | async-start | bytes 8388608
  243.5 210.9 %reduce-scatter.5.cloned.1.call-start = ((), (), s32[]{:S(2)}) async-start(), calls=%async_computation.5 | async-start | bytes 2211840 | tf_op jit(solution)/shard_map/reduce_scatter | solution.py:750
  250.8 22.2 %collective-permute-start.4 = (bf16[2,1,14,768]{3,2,1,0:T(8,128)(2,1)S(1)}, bf16[2,1,14,768]{3,2,1,0:T(8,128)(2,1)S(1)}, u32[]{:S(2)}, u32[]{:S(2)}) collective-permute-start(bf16[2,1,14,768]{3,2,1,0:T(8,128)(2,1)S(1)} %fusion.112), channel_id=1, source_target_pairs={{0,2},{1,3},{2,0},{3,1},{4,6},{5,7},{6,4},{7,5},{8,10},{9,11},{10,... | collective-permute-start | bytes 129032 | tf_op jit(solution)/shard_map/ppermute | solution.py:19
  274.1 7.5 %collective-permute-start.5 = (bf16[2,12,1,768]{3,2,1,0:T(2,128)(2,1)}, bf16[2,12,1,768]{3,2,1,0:T(2,128)(2,1)}, u32[]{:S(2)}, u32[]{:S(2)}) collective-permute-start(bf16[2,12,1,768]{3,2,1,0:T(2,128)(2,1)} %fusion.113), channel_id=1, source_target_pairs={{0,1},{1,0},{2,3},{3,2},{4,5},{5,4},{6,7},{7,6},{8,9},{9,8},{10,11... | collective-permute-start | bytes 110600 | tf_op jit(solution)/shard_map/ppermute | solution.py:19
  296.6 21.8 %slice-start.8 = ((s8[8388608]{0:T(1024)(128)(4,1)}), s8[4194304]{0:T(1024)(128)(4,1)S(1)}, s32[]{:S(2)}) async-start(s8[8388608]{0:T(1024)(128)(4,1)} %bitcast.311), calls=%async_computation.14 | async-start | bytes 8388608
  300.8 17.6 %slice-start.9 = ((s8[8388608]{0:T(1024)(128)(4,1)}), s8[4194304]{0:T(1024)(128)(4,1)S(1)}, s32[]{:S(2)}) async-start(s8[8388608]{0:T(1024)(128)(4,1)} %bitcast.311), calls=%async_computation.15 | async-start | bytes 8388608
  318.5 19.6 %copy-start.4 = (f32[2,24,24,1024]{3,2,1,0:T(8,128)S(1)}, f32[2,24,24,1024]{3,2,1,0:T(8,128)}, u32[]{:S(2)}) copy-start(f32[2,24,24,1024]{3,2,1,0:T(8,128)} %depthwise_seven.2) | copy-start | bytes 14155780
  318.5 19.6 %copy-start.54 = (f32[2,24,24]{2,1,0:T(8,128)S(1)}, f32[2,24,24]{2,1,0:T(8,128)}, u32[]{:S(2)}) copy-start(f32[2,24,24]{2,1,0:T(8,128)} %copy-done.53) | copy-start | bytes 13828
  318.5 19.6 %copy-start.76 = (f32[1024]{0:T(1024)S(1)}, f32[1024]{0:T(1024)}, u32[]{:S(2)}) copy-start(f32[1024]{0:T(1024)} %copy-done.75) | copy-start | bytes 12292
  338.1 16.6 %copy-start.58 = (f32[2,24,24]{2,1,0:T(8,128)S(1)}, f32[2,24,24]{2,1,0:T(8,128)}, u32[]{:S(2)}) copy-start(f32[2,24,24]{2,1,0:T(8,128)} %copy-done.57) | copy-start | bytes 13828
  338.1 16.6 %copy-start.60 = (f32[2,24,24]{2,1,0:T(8,128)S(1)}, f32[2,24,24]{2,1,0:T(8,128)}, u32[]{:S(2)}) copy-start(f32[2,24,24]{2,1,0:T(8,128)} %copy-done.59) | copy-start | bytes 13828
  362.4 18.7 %copy-start.24 = (bf16[2,24,3,1024]{3,2,1,0:T(4,128)(2,1)S(1)}, bf16[2,24,3,1024]{3,2,1,0:T(4,128)(2,1)}, u32[]{:S(2)}) copy-start(bf16[2,24,3,1024]{3,2,1,0:T(4,128)(2,1)} %copy-done.23) | copy-start | bytes 884740
  362.4 18.6 %collective-permute-start.6 = (bf16[2,24,3,1024]{3,2,1,0:T(4,128)(2,1)S(1)}, bf16[2,24,3,1024]{3,2,1,0:T(4,128)(2,1)S(1)}, u32[]{:S(2)}, u32[]{:S(2)}) collective-permute-start(bf16[2,24,3,1024]{3,2,1,0:T(4,128)(2,1)S(1)} %slice_select_fusion.1), channel_id=1, source_target_pairs={{0,1},{1,0},{2,3},{3,2},{4,5},{5,4},{6,7},{7,6},{8,9},{9,8},{10,11... | collective-permute-start | bytes 884744 | tf_op jit(solution)/shard_map/ppermute | solution.py:19
  383.4 28.6 %collective-permute-start.7 = (bf16[2,3,30,1024]{3,2,1,0:T(8,128)(2,1)S(1)}, bf16[2,3,30,1024]{3,2,1,0:T(8,128)(2,1)S(1)}, u32[]{:S(2)}, u32[]{:S(2)}) collective-permute-start(bf16[2,3,30,1024]{3,2,1,0:T(8,128)(2,1)S(1)} %slice_select_fusion), channel_id=1, source_target_pairs={{0,2},{1,3},{2,0},{3,1},{4,6},{5,7},{6,4},{7,5},{8,10},{9,11},{10,... | collective-permute-start | bytes 1105928 | tf_op jit(solution)/shard_map/ppermute | solution.py:19
  387.5 24.5 %copy-start.22 = (bf16[2,3,30,1024]{3,2,1,0:T(8,128)(2,1)S(1)}, bf16[2,3,30,1024]{3,2,1,0:T(8,128)(2,1)}, u32[]{:S(2)}) copy-start(bf16[2,3,30,1024]{3,2,1,0:T(8,128)(2,1)} %copy-done.21) | copy-start | bytes 1105924
  415.8 25.5 %copy-start.96 = (f32[2]{0:T(128)S(1)}, f32[2]{0:T(128)}, u32[]{:S(2)}) copy-start(f32[2]{0:T(128)} %copy-done.93) | copy-start | bytes 28
  441.4 13.0 %copy-start.12 = (bf16[2,1,144,768]{3,2,1,0:T(8,128)(2,1)S(1)}, bf16[2,1,144,768]{3,2,1,0:T(8,128)(2,1)}, u32[]{:S(2)}) copy-start(bf16[2,1,144,768]{3,2,1,0:T(8,128)(2,1)} %param.21) | copy-start | bytes 1327108
  441.4 12.9 %copy-start.70 = (f32[768]{0:T(1024)S(1)}, f32[768]{0:T(1024)}, u32[]{:S(2)}) copy-start(f32[768]{0:T(1024)} %copy-done.68) | copy-start | bytes 9220
  441.4 12.9 %copy-start.73 = (f32[2,144]{1,0:T(2,128)S(1)}, f32[2,144]{1,0:T(2,128)}, u32[]{:S(2)}) copy-start(f32[2,144]{1,0:T(2,128)} %copy-done.71) | copy-start | bytes 3460
  618.8 17.1 %copy-start.64 = (f32[96,192]{1,0:T(8,128)S(1)}, f32[96,192]{1,0:T(8,128)}, u32[]{:S(2)}) copy-start(f32[96,192]{1,0:T(8,128)} %get-tuple-element.193) | copy-start | bytes 221188
  618.8 21.0 %copy-start.1 = (bf16[1024,768]{1,0:T(8,128)(2,1)S(1)}, bf16[1024,768]{1,0:T(8,128)(2,1)}, u32[]{:S(2)}) copy-start(bf16[1024,768]{1,0:T(8,128)(2,1)} %param.34) | copy-start | bytes 4718596
  624.1 15.0 %copy-start.48 = (f32[512,256]{1,0:T(8,128)S(1)}, f32[512,256]{1,0:T(8,128)}, u32[]{:S(2)}) copy-start(f32[512,256]{1,0:T(8,128)} %get-tuple-element.197) | copy-start | bytes 1572868
  (87 other events, 456.8 us)
Sparse Core Ops, SparseCore 0:
  14.0 59.1 all-gather.4
  75.4 38.4 all-gather.2
  243.6 40.5 reduce-scatter.2
  286.4 38.0 reduce-scatter.4
